TPU v7x, 512 devices: a whole 4x8x8 slice. The times are simulated.
512 devices in a mesh: req: 128 (over z, y, core), head: 4 (over x).
Axes of the slice: x: 4, y: 8, z: 8, core: 2. Of those that a mesh axis runs over, the one named last changes fastest.
Arguments:
- hidden_in: bfloat16 [256, 2048], P(None, 'head'), may hold values from -1.5 to 1.5
- attention_gain: float32 [2048], replicated, may hold values from 0.1 to 1.9
- query_gain: float32 [64], replicated, may hold values from 0.5 to 2
- key_gain: float32 [64], replicated, may hold values from 1.5 to 4
- feedforward_gain: float32 [2048], replicated, may hold values from 0.1 to 1.9
- input_weight: bfloat16 [2048, 1920], P('req', 'head'), may hold values from -0.125 to 0.125
- output_weight: bfloat16 [1280, 2048], P('req', 'head'), may hold values from -0.15625 to 0.15625
- gate_weight: bfloat16 [2048, 5120], P('req', 'head'), may hold values from -0.125 to 0.125
- up_weight: bfloat16 [2048, 5120], P('req', 'head'), may hold values from -0.125 to 0.125
- down_weight: bfloat16 [5120, 2048], P('req', 'head'), may hold values from -0.078125 to 0.078125
- old_cache: bfloat16 [4096, 128, 640], P(('req', 'head')), may hold values from -400 to 400
- keep_rows: int32 [4096, 64], P(('req', 'head')), may hold values from -1 to 127, as said below
- drop_weights: float32 [4096, 128], P(('req', 'head')), may hold values from 0.1 to 1
- dest_slots: int32 [512, 8], P(('req', 'head')), may hold values from 0 to 7, each once within a row
- lengths: int32 [256], replicated, may hold values from 1 to 16, 2048 in all
- page_table: int32 [256, 16], P('req'), may hold values from 0 to 7, as said below
- source: int32 [128], replicated, may hold values from 0 to 127, each once
Outputs:
- compact_cache: bfloat16 [2048, 128, 640], P(('req', 'head'))
- summary_rows: bfloat16 [4096, 640], P(('req', 'head'))
- hidden_out: bfloat16 [256, 2048], P(None, 'head')
Inputs may be any that keep to these rules, and one draw needn't show every extreme that they name: `keep_rows`: row p lists kept rows of page p in ascending order, from 32 to 64 of them, then -1 to the end; some page keeps 64. `page_table`: row g * 2 + k belongs to the k-th request held by index g of req; entry j is the slot, on the device with req index g and head index j % 4, of that request's j-th page. On every device the entries that point to it form a permutation of its 8 slots. `source`: A permutation of the continued requests over the held slots. `dest_slots`: each row is a permutation. `lengths`: they sum to 2048 and the largest is 16.
All inputs are finite; a program needn't handle non-finite values.
Results may differ from a plain program's by a relative error of at most 0.015.
The roundings to bfloat16 on the way count: a program that leaves them out, or rounds other values in their place, can miss the bound.
Values may be sent and summed in bfloat16 or wider, within the bound.
A program may use at most 64 MiB of HBM per device.

v0:
```python
import jax
import jax.numpy as jnp
from jax import lax
from jax.sharding import PartitionSpec as P

D = 2048
HEADS = 20
KVH = 5
HD = 64
FF = 5120
PAGE = 128
KEEP = 64
NP = 16
R_DEV = 2
KVW = 640


epsilon = 1e-06
negative = -1e30


def joined(part, axis, combine):
    gathered = jax.tree.map(lambda a: lax.all_gather(a, axis), part)

    def take(source):
        return jax.tree.map(lambda a: lax.dynamic_index_in_dim(a, source, 0, False), gathered)

    return lax.fori_loop(
        1, lax.axis_size(axis), lambda source, state: combine(state, take(source)), take(0)
    )


def rms_rows(values, gain):
    mean_square = jnp.mean(values * values, axis=-1, keepdims=True)
    return values * lax.rsqrt(mean_square + epsilon) * gain


def rotate(vectors, positions):
    half = vectors.shape[-1] // 2
    frequency = 10000.0 ** (-jnp.arange(half, dtype=jnp.float32) / half)
    angles = positions.astype(jnp.float32)[:, None] * frequency[None, :]
    cosine = jnp.cos(angles)[:, None, :]
    sine = jnp.sin(angles)[:, None, :]
    first = vectors[..., :half]
    second = vectors[..., half:]
    return jnp.concatenate(
        [first * cosine - second * sine, second * cosine + first * sine], axis=-1
    )


def compact_pages(pages, keep, weights):
    rows = jnp.arange(pages.shape[1], dtype=jnp.int32)
    picks = keep[:, :, None] == rows[None, None, :]
    kept = jnp.einsum(
        "pkr,prc->pkc", picks.astype(jnp.bfloat16), pages, preferred_element_type=jnp.float32
    ).astype(jnp.bfloat16)
    dropped = weights * (1.0 - jnp.sum(picks.astype(jnp.float32), axis=1))
    total = jnp.sum(dropped, axis=1)
    means = (
        jnp.einsum(
            "pr,prc->pc", dropped, pages.astype(jnp.float32), precision=lax.Precision.HIGHEST
        )
        / total[:, None]
    )
    return (kept, means.astype(jnp.bfloat16), jnp.log(total))


def merge_parts(first, second):
    top_first, mass_first, sum_first = first
    top_second, mass_second, sum_second = second
    top = jnp.maximum(top_first, top_second)
    scale_first = jnp.exp(top_first - top)
    scale_second = jnp.exp(top_second - top)
    mass = mass_first * scale_first + mass_second * scale_second
    summed = sum_first * scale_first[..., None] + sum_second * scale_second[..., None]
    return (top, mass, summed)


def held_request(rows, source):
    half = R_DEV // 2
    position = rows % R_DEV
    slot = rows // R_DEV * half + position - half
    continued = jnp.arange(source.shape[0], dtype=jnp.int32)
    matches = source[None, :] == slot[:, None]
    owner_cont = jnp.sum(jnp.where(matches, continued[None, :], 0), axis=1)
    carried = owner_cont // half * R_DEV + half + owner_cont % half
    return jnp.where(position < half, rows, carried)


def full_rows(values):
    return lax.all_gather(values, "head", axis=1, tiled=True)


def feature_block(rows, count):
    return lax.dynamic_slice_in_dim(rows, lax.axis_index("req") * count, count, 1)


def normed_block(rows, gain, count):
    whole = full_rows(rows)
    normed = rms_rows(whole.astype(jnp.float32), gain).astype(jnp.bfloat16)
    return feature_block(normed, count)


def input_block(rows, count):
    return feature_block(full_rows(rows), count)


def project(inputs, weight):
    return lax.psum(jnp.dot(inputs, weight, preferred_element_type=jnp.float32), "req")


def on_device(
    hidden_in,
    attention_gain,
    query_gain,
    key_gain,
    feedforward_gain,
    input_weight,
    output_weight,
    gate_weight,
    up_weight,
    down_weight,
    old_cache,
    keep_rows,
    drop_weights,
    dest_slots,
    lengths,
    page_table,
    source,
):
    groups = lax.axis_size("req")
    lanes = lax.axis_size("head")
    group = lax.axis_index("req")
    lane = lax.axis_index("head")
    requests = hidden_in.shape[0]
    half = R_DEV // 2
    split = KVH * HD
    ratio = HEADS // KVH
    scale = HD ** (-0.5)
    pages_here = old_cache.shape[0]
    slots = jnp.arange(R_DEV, dtype=jnp.int32)
    held = held_request(group * R_DEV + slots, source)
    held_len = lengths[held]
    positions = held_len * PAGE
    inputs = normed_block(hidden_in, attention_gain, D // groups)
    partial_qkv = jnp.dot(inputs, input_weight, preferred_element_type=jnp.float32)
    mixed = lax.psum(partial_qkv, "req").astype(jnp.bfloat16)
    qkv = lax.all_gather(mixed, "head", axis=1, tiled=True)
    held_qkv = qkv[held].astype(jnp.float32)
    query = rotate(
        rms_rows(held_qkv[:, : HEADS * HD].reshape(R_DEV, HEADS, HD), query_gain), positions
    ).astype(jnp.bfloat16)
    key_new = rotate(
        rms_rows(held_qkv[:, HEADS * HD : (HEADS + KVH) * HD].reshape(R_DEV, KVH, HD), key_gain),
        positions,
    ).astype(jnp.bfloat16)
    value_new = held_qkv[:, (HEADS + KVH) * HD :].reshape(R_DEV, KVH, HD)
    kept, means, bias = compact_pages(old_cache, keep_rows, drop_weights)
    destination = dest_slots[0]
    fresh_ids = jnp.arange(pages_here, dtype=jnp.int32)
    inverse = jnp.sum(
        jnp.where(destination[None, :] == fresh_ids[:, None], fresh_ids[None, :], 0), axis=1
    )
    compact = kept[inverse].reshape(pages_here // 2, PAGE, KVW)
    summaries = means[inverse]
    per_lane = NP // lanes
    table = page_table.reshape(R_DEV, per_lane, lanes)
    mine = lax.dynamic_slice_in_dim(table, lane, 1, 2)[:, :, 0]
    logical = jnp.arange(per_lane, dtype=jnp.int32) * lanes + lane
    live = logical[None, :] < held_len[:, None]
    owner = jnp.any((mine[:, :, None] == fresh_ids[None, None, :]) & live[:, :, None], axis=1)
    query_groups = query.reshape(R_DEV, KVH, ratio, HD)
    row_keys = kept[:, :, :split].reshape(pages_here, KEEP, KVH, HD)
    row_values = kept[:, :, split:].reshape(pages_here, KEEP, KVH, HD)
    row_live = keep_rows >= 0
    allowed = owner[:, None, None, :, None] & row_live[None, None, None, :, :]
    scores = (
        jnp.einsum("rngd,pmnd->rngpm", query_groups, row_keys, preferred_element_type=jnp.float32)
        * scale
    )
    scores = jnp.where(allowed, scores, negative)
    mean_keys = means[:, :split].reshape(pages_here, KVH, HD)
    mean_values = means[:, split:].reshape(pages_here, KVH, HD)
    mean_scores = (
        jnp.einsum("rngd,pnd->rngp", query_groups, mean_keys, preferred_element_type=jnp.float32)
        * scale
        + bias[None, None, None, :]
    )
    mean_allowed = owner[:, None, None, :]
    mean_scores = jnp.where(mean_allowed, mean_scores, negative)
    top = jnp.maximum(jnp.max(scores, axis=(3, 4)), jnp.max(mean_scores, axis=3))
    row_weight = jnp.where(allowed, jnp.exp(scores - top[..., None, None]), 0.0)
    mean_weight = jnp.where(mean_allowed, jnp.exp(mean_scores - top[..., None]), 0.0)
    mass = jnp.sum(row_weight, axis=(3, 4)) + jnp.sum(mean_weight, axis=3)
    total = jnp.einsum(
        "rngpm,pmnd->rngd",
        row_weight,
        row_values.astype(jnp.float32),
        precision=lax.Precision.HIGHEST,
    )
    total = total + jnp.einsum(
        "rngp,pnd->rngd",
        mean_weight,
        mean_values.astype(jnp.float32),
        precision=lax.Precision.HIGHEST,
    )
    top, mass, total = joined((top, mass, total), "head", merge_parts)
    own_score = (
        jnp.einsum("rngd,rnd->rng", query_groups, key_new, preferred_element_type=jnp.float32)
        * scale
    )
    final_top = jnp.maximum(top, own_score)
    earlier = jnp.exp(top - final_top)
    own_weight = jnp.exp(own_score - final_top)
    mass = mass * earlier + own_weight
    total = total * earlier[..., None] + own_weight[..., None] * value_new[:, :, None, :]
    attention = (total / mass[..., None]).reshape(R_DEV, HEADS * HD).astype(jnp.bfloat16)
    moved = lax.all_to_all(attention, "req", split_axis=1, concat_axis=0, tiled=True)
    everyone = jnp.arange(requests, dtype=jnp.int32)
    position = everyone % R_DEV
    cont_index = everyone // R_DEV * half + position - half
    slot_of = source[jnp.clip(cont_index, 0, source.shape[0] - 1)]
    held_row = slot_of // half * R_DEV + half + slot_of % half
    row_of = jnp.where(position < half, everyone, held_row)
    attention_rows = moved[row_of]
    projected = project(attention_rows, output_weight)
    mid = (hidden_in.astype(jnp.float32) + projected).astype(jnp.bfloat16)
    inputs_mid = normed_block(mid, feedforward_gain, D // groups)
    both = jnp.concatenate([gate_weight, up_weight], axis=1)
    local_units = gate_weight.shape[1]
    sums = lax.psum(jnp.dot(inputs_mid, both, preferred_element_type=jnp.float32), "req")
    active = (jax.nn.silu(sums[:, :local_units]) * sums[:, local_units:]).astype(jnp.bfloat16)
    down = project(input_block(active, FF // groups), down_weight)
    residual = lax.optimization_barrier(mid).astype(jnp.float32)
    result = (residual + down).astype(jnp.bfloat16)
    return (compact, summaries, result)


def solution(mesh):
    placed = (
        P(None, "head"),
        P(),
        P(),
        P(),
        P(),
        P("req", "head"),
        P("req", "head"),
        P("req", "head"),
        P("req", "head"),
        P("req", "head"),
        P(("req", "head"), None, None),
        P(("req", "head"), None),
        P(("req", "head"), None),
        P(("req", "head"), None),
        P(),
        P("req", None),
        P(),
    )
    return jax.shard_map(
        on_device,
        mesh=mesh,
        in_specs=placed,
        out_specs=(P(("req", "head"), None, None), P(("req", "head"), None), P(None, "head")),
        check_vma=False,
    )
```

profile of v0, /device:TPU:1, one launch (start us, length us, event | category | flops | bytes accessed | tf_op | source)
XLA Modules:
  0.0 1285.9 jit_solution(14385195051736186096)
XLA Ops:
  8.8 1.9 gather_fusion.4
  20.6 23.4 %all-gather.7.cloned.1.call-done = bf16[256,2048]{1,0:T(8,128)(2,1)} async-done(((bf16[256,512]{1,0:T(8,128)(2,1)}), bf16[256,2048]{1,0:T(8,128)(2,1)}) %all-gather.7.cloned.1.call-update) | async-done | bytes 1048592 | tf_op jit(solution)/shard_map/all_gather | solution.py:91
  44.0 1.5 multiply_reduce_fusion.1
  45.5 1.5 convert_element_type.68
  47.4 491.6 %all-reduce.10 = bf16[256,480]{0,1:T(8,128)(2,1)S(1)} all-reduce(f32[256,480]{0,1:T(8,128)S(1)} %fusion.23), channel_id=1, replica_groups=mesh['req'=128,'head'=4] {'req'}, use_global_device_ids=true, to_apply=%region_6.7 | all-reduce | flops 122880 | bytes 737280 | tf_op jit(solution)/shard_map/psum | solution.py:147
  539.1 12.2 all_gather.27
  552.7 2.0 gather_fusion.3
  558.2 9.0 all-gather.1
  567.2 9.0 all-gather
  577.1 9.0 all-gather.2
  588.5 21.7 %all-to-all-start = ((bf16[2,128,10]{2,0,1:T(2,128)(2,1)}), bf16[2,128,10]{2,0,1:T(2,128)(2,1)S(1)}, u32[]{:S(2)}, u32[]{:S(2)}) async-start(bf16[2,128,10]{2,0,1:T(2,128)(2,1)} %copy.103), calls=%async_computation | async-start | bytes 131072 | tf_op jit(solution)/shard_map/all_to_all | solution.py:218
  610.3 11.4 all-to-all-done
  623.6 181.6 %all-reduce.5.cloned.1.call-done = f32[256,512]{1,0:T(8,128)} async-done(((f32[256,512]{1,0:T(8,128)}), f32[256,512]{1,0:T(8,128)}) %all-reduce.5.cloned.1.call-update) | async-done | bytes 524304 | tf_op jit(solution)/shard_map/psum | solution.py:109
  805.2 1.8 add_convert_fusion.1
  807.8 26.2 %all-gather.9.cloned.1.call-done = bf16[256,2048]{1,0:T(8,128)(2,1)} async-done(((bf16[256,512]{1,0:T(8,128)(2,1)}), bf16[256,2048]{1,0:T(8,128)(2,1)}) %all-gather.9.cloned.1.call-update) | async-done | bytes 1048592 | tf_op jit(solution)/shard_map/all_gather | solution.py:91
  834.0 1.5 multiply_reduce_fusion
  837.0 2.1 fusion.19
  839.2 202.1 %all-reduce.7.cloned.1.call-done = f32[256,2560]{1,0:T(8,128)} async-done(((f32[256,2560]{1,0:T(8,128)}), f32[256,2560]{1,0:T(8,128)}) %all-reduce.7.cloned.1.call-update) | async-done | bytes 2621456 | tf_op jit(solution)/shard_map/psum | solution.py:231
  1041.3 2.9 fusion.4
  1044.4 38.3 %all-gather.11.cloned.1.call-done = bf16[256,5120]{1,0:T(8,128)(2,1)} async-done(((bf16[256,1280]{1,0:T(8,128)(2,1)}), bf16[256,5120]{1,0:T(8,128)(2,1)}) %all-gather.11.cloned.1.call-update) | async-done | bytes 2621456 | tf_op jit(solution)/shard_map/all_gather | solution.py:91
  1082.7 2.0 fusion.30
  1085.9 1.5 gather_fusion
  1087.4 189.9 %all-reduce.9.cloned.1.call-done = f32[256,512]{1,0:T(8,128)} async-done(((f32[256,512]{1,0:T(8,128)}), f32[256,512]{1,0:T(8,128)}) %all-reduce.9.cloned.1.call-update) | async-done | bytes 524304 | tf_op jit(solution)/shard_map/psum | solution.py:109
  1277.2 1.8 add_convert_fusion
  (139 shorter events, 26.6 us)
Async XLA Ops:
  7.2 7.8 copy-start
  7.2 36.8 %all-gather.7.cloned.1.call-start = ((), (), s32[]{:S(2)}) async-start(), calls=%async_computation.1 | async-start | bytes 1310720 | tf_op jit(solution)/shard_map/all_gather | solution.py:91
  16.8 3.7 copy-start.7
  20.6 26.4 %copy-start.8 = (bf16[16,480]{1,0:T(8,128)(2,1)S(1)}, bf16[16,480]{1,0:T(8,128)(2,1)}, u32[]{:S(2)}) copy-start(bf16[16,480]{1,0:T(8,128)(2,1)} %param.24) | copy-start | bytes 46084
  47.4 507.7 %copy-start.11 = (f32[64]{0:T(128)S(1)}, f32[64]{0:T(128)}, u32[]{:S(2)}) copy-start(f32[64]{0:T(128)} %param.22) | copy-start | bytes 772
  47.4 507.8 %copy-start.10 = (f32[64]{0:T(128)S(1)}, f32[64]{0:T(128)}, u32[]{:S(2)}) copy-start(f32[64]{0:T(128)} %param.21) | copy-start | bytes 772
  552.7 23.6 %copy-start.3 = (bf16[8,64,320]{1,2,0:T(8,128)(2,1)S(1)}, bf16[8,64,320]{1,2,0:T(8,128)(2,1)}, u32[]{:S(2)}) copy-start(bf16[8,64,320]{1,2,0:T(8,128)(2,1)} %copy.94) | copy-start | bytes 983044
  557.3 65.2 %copy-start.9 = (bf16[10,512]{1,0:T(8,128)(2,1)S(1)}, bf16[10,512]{1,0:T(8,128)(2,1)}, u32[]{:S(2)}) copy-start(bf16[10,512]{1,0:T(8,128)(2,1)} %param.25) | copy-start | bytes 30724
  576.2 228.9 %copy-start.2 = (bf16[256,512]{1,0:T(8,128)(2,1)S(1)}, bf16[256,512]{1,0:T(8,128)(2,1)}, u32[]{:S(2)}) copy-start(bf16[256,512]{1,0:T(8,128)(2,1)} %param.19) | copy-start | bytes 786436
  588.5 33.2 %all-to-all-start = ((bf16[2,128,10]{2,0,1:T(2,128)(2,1)}), bf16[2,128,10]{2,0,1:T(2,128)(2,1)S(1)}, u32[]{:S(2)}, u32[]{:S(2)}) async-start(bf16[2,128,10]{2,0,1:T(2,128)(2,1)} %copy.103), calls=%async_computation | async-start | bytes 131072 | tf_op jit(solution)/shard_map/all_to_all | solution.py:218
  610.2 195.0 %all-reduce.5.cloned.1.call-start = ((), (), s32[]{:S(2)}) async-start(), calls=%async_computation.2 | async-start | bytes 1048576 | tf_op jit(solution)/shard_map/psum | solution.py:109
  623.6 210.5 %all-gather.9.cloned.1.call-start = ((), (), s32[]{:S(2)}) async-start(), calls=%async_computation.3 | async-start | bytes 1310720 | tf_op jit(solution)/shard_map/all_gather | solution.py:91
  807.0 234.3 %all-reduce.7.cloned.1.call-start = ((), (), s32[]{:S(2)}) async-start(), calls=%async_computation.4 | async-start | bytes 5242880 | tf_op jit(solution)/shard_map/psum | solution.py:231
  807.8 29.2 %copy-start.5 = (bf16[16,1280]{1,0:T(8,128)(2,1)S(1)}, bf16[16,1280]{1,0:T(8,128)(2,1)}, u32[]{:S(2)}) copy-start(bf16[16,1280]{1,0:T(8,128)(2,1)} %param.27) | copy-start | bytes 122884
  807.8 29.2 %copy-start.6 = (bf16[16,1280]{1,0:T(8,128)(2,1)S(1)}, bf16[16,1280]{1,0:T(8,128)(2,1)}, u32[]{:S(2)}) copy-start(bf16[16,1280]{1,0:T(8,128)(2,1)} %param.26) | copy-start | bytes 122884
  839.2 205.1 %copy-start.12 = (s32[1,8]{1,0:T(1,128)S(1)}, s32[1,8]{1,0:T(1,128)}, u32[]{:S(2)}) copy-start(s32[1,8]{1,0:T(1,128)} %param.32) | copy-start | bytes 100
  839.2 243.5 %copy-start.4 = (bf16[40,512]{1,0:T(8,128)(2,1)S(1)}, bf16[40,512]{1,0:T(8,128)(2,1)}, u32[]{:S(2)}) copy-start(bf16[40,512]{1,0:T(8,128)(2,1)} %param.28) | copy-start | bytes 122884
  839.2 243.5 %all-gather.11.cloned.1.call-start = ((), (), s32[]{:S(2)}) async-start(), calls=%async_computation.5 | async-start | bytes 3276800 | tf_op jit(solution)/shard_map/all_gather | solution.py:91
  1044.2 233.0 %copy-start.1 = (bf16[256,512]{1,0:T(8,128)(2,1)S(1)}, bf16[256,512]{1,0:T(8,128)(2,1)}, u32[]{:S(2)}) copy-start(bf16[256,512]{1,0:T(8,128)(2,1)} %add_convert_fusion.1) | copy-start | bytes 786436
  1044.2 233.0 %all-reduce.9.cloned.1.call-start = ((), (), s32[]{:S(2)}) async-start(), calls=%async_computation.6 | async-start | bytes 1048576 | tf_op jit(solution)/shard_map/psum | solution.py:109
Sparse Core Ops, SparseCore 0:
  10.1 33.8 all-gather.6
  623.7 181.4 all-reduce.4
  807.8 26.1 all-gather.8
  839.3 201.9 all-reduce.6
  1044.3 38.2 all-gather.10
  1086.1 191.0 all-reduce.8
where the time goes:
time: 1290 us
  waiting for transfers between devices  674 us (52%)
  blocking collectives  531 us (41%)
  starting transfers between devices  21.9 us (2%)
  local copies, waits for them, and re-layouts  17.8 us (1%)
  other arithmetic  17.2 us (1%)
  between operations  14.5 us (1%)
    psum x1, blocking collectives, on_device(): mixed = lax.psum(partial_qkv, 'req').astype(jnp.bfloat16)  492 us
    psum x2, waiting for transfers between devices, project(): lax.psum(jnp.dot(inputs, weight, preferred_element_type=jnp.float32), 'req')  371 us
    psum x1, waiting for transfers between devices, on_device(): lax.psum(jnp.dot(inputs_mid, both, preferred_element_type=jnp.float32), '...  202 us
    all_gather x3, waiting for transfers between devices, full_rows(): return lax.all_gather(values, 'head', axis=1, tiled=True)  87.9 us
    all_gather x3, blocking collectives, joined(): gathered = jax.tree.map(lambda a: lax.all_gather(a, axis), part)  27.1 us
  transfers between devices with their start and end apart: 7, of which 7 were waited for; matrix products, arithmetic and copies ran while one was open for 1% of the time, Pallas kernels for 0%

commit v1 on v0

v1 whole, which is shorter than its diff:
```python
import jax
import jax.numpy as jnp
from jax import lax
from jax.experimental import pallas as pl
from jax.experimental.pallas import tpu as pltpu
from jax.sharding import PartitionSpec as P

D = 2048
HEADS = 20
KVH = 5
HD = 64
PAGE = 128
KEEP = 64
NP = 16
R_DEV = 2
KVW = 640
QROWS = 24

epsilon = 1e-06
negative = -1e30
bf16 = jnp.bfloat16
f32 = jnp.float32
i32 = jnp.int32


def iota(shape, dim):
    return lax.broadcasted_iota(i32, shape, dim)


def dot(a, b):
    return jnp.dot(a, b, preferred_element_type=f32)


def dot_t(a, b):
    return lax.dot_general(a, b, (((1,), (1,)), ((), ())), preferred_element_type=f32)


def rounded(values):
    return values.astype(bf16).astype(f32)


def at_lane(values, lane):
    return jnp.sum(jnp.where(iota(values.shape, 1) == lane, values, 0.0), axis=1, keepdims=True)


def kernel(
    hidden_ref, held_ref, win_ref, wo_ref, wg_ref, wu_ref, wd_ref,
    cache_ref, keep_ref, drop_ref, inv_ref, cos_ref, sin_ref, allow_ref,
    again_ref, fgain_ref, qgain_ref, kgain_ref,
    compact_ref, summary_ref, out_ref,
    hx, win_s, wo_s, gu_s, wd_s, win_w, wo_w, gu_w, wd_w,
    pb, rb, cx, fa, kv, tail, dx, eb, ex, xa, ox, mx, mid_f, gs, gx, ax, ys, yx, jx, sumr, means,
    s_w1, r_w1, s_z, r_z, s_ring, r_ring, s_ph, r_ph,
):
    group = lax.axis_index("req")
    x = lax.axis_index("head")
    z = group // 16
    yc = lax.rem(group, 16)
    ya = yc // 4
    yb = lax.rem(yc, 4)
    y = yc // 2
    c = lax.rem(yc, 2)
    col = x * 4 + ya

    def dev(zz, yy, xx):
        return {"req": zz * 16 + yy, "head": xx}

    def remote(src, dst, ssem, rsem, target):
        return pltpu.make_async_remote_copy(
            src_ref=src, dst_ref=dst, send_sem=ssem, recv_sem=rsem,
            device_id=target, device_id_type=pl.DeviceIdType.MESH,
        )

    def yc_peer(j):
        return lax.rem(yc + j, 16)

    def col_peer(j):
        return lax.rem(col + j, 16)

    def x_peer(j):
        return lax.rem(x + j, 4)

    def yb_peer(j):
        return lax.rem(yb + j, 4)

    def z_peer(j):
        return lax.rem(z + j, 8)

    wd_w[:, :, 6:8] = jnp.zeros((8, 2, 2, 16, 128), bf16)

    barrier = pltpu.get_barrier_semaphore()

    def greet(target):
        pl.semaphore_signal(barrier, inc=1, device_id=target, device_id_type=pl.DeviceIdType.MESH)

    @pl.loop(1, 16)
    def _(j):
        greet(dev(z, yc_peer(j), x))

    @pl.loop(0, 12)
    def _(j):
        greet(dev(z, (j // 3) * 4 + yb, x_peer(1 + lax.rem(j, 3))))

    @pl.loop(1, 8)
    def _(j):
        greet(dev(z_peer(j), yc, x))

    win = win_ref[...]
    pad = jnp.zeros((16, 32), bf16)
    even = jnp.concatenate([win, pad], axis=1)
    odd = jnp.concatenate([pad, win], axis=1)
    shifted = jnp.where(lax.rem(x, 2) == 0, even, odd)
    wo_s[...] = jnp.zeros_like(wo_s)
    wd_s[...] = jnp.zeros_like(wd_s)
    gu_s[...] = jnp.zeros_like(gu_s)
    wo_full = jnp.concatenate([wo_ref[...], jnp.zeros((6, 512), bf16)], axis=0)
    wd_full = jnp.concatenate([wd_ref[...], jnp.zeros((8, 512), bf16)], axis=0)
    gate = wg_ref[...]
    up = wu_ref[...]
    for a in range(4):
        lanes = slice(a * 128, (a + 1) * 128)
        win_s[a] = shifted[:, lanes]
        wo_s[a] = wo_full[:, lanes]
        for k in range(3):
            wd_s[a, k] = wd_full[k * 16:(k + 1) * 16, lanes]
        for k in range(4):
            for h in range(2):
                first = a * 320 + k * 80 + h * 40
                gu_s[a, :, k * 256 + h * 48:k * 256 + h * 48 + 40] = gate[:, first:first + 40]
                gu_s[a, :, k * 256 + 128 + h * 48:k * 256 + 128 + h * 48 + 40] = up[:, first:first + 40]

    chosen = (held_ref[...] == iota((32, 256), 1)).astype(bf16)
    rows_here = dot(chosen, hidden_ref[...]).astype(bf16)
    hx[x] = rows_here

    pl.semaphore_wait(barrier, 34)

    def h_copy(j):
        return remote(hx.at[x], hx.at[x], s_ph.at[0], r_ph.at[0], dev(z, yc, x_peer(j)))

    cls = lax.rem(y, 4)
    yh = y // 4
    slot = yh * 2 + c

    def w1_parts(a):
        return (
            (win_s.at[a], win_w.at[z, slot], 0),
            (wo_s.at[a], wo_w.at[z, slot], 1),
            (gu_s.at[a], gu_w.at[z, slot], 2),
            (wd_s.at[a], wd_w.at[z, yh, pl.ds(c * 3, 3)], 3),
        )

    for m in range(4):
        for a in range(4):
            src, dst, which = w1_parts(a)[m]
            target = a * 4 + cls

            @pl.when(target != yc)
            def _():
                remote(src, dst, s_w1.at[which, a], r_w1.at[which], dev(z, target, x)).start()

            @pl.when(target == yc)
            def _():
                pltpu.make_async_copy(src, dst, r_w1.at[which]).start()

        if m == 0:
            for j in range(1, 4):
                h_copy(j).start()

    def w1_wait(which, block):
        pltpu.make_async_copy(block, block, r_w1.at[which]).wait()

    def z_copy(which, buf, j):
        return remote(buf.at[z], buf.at[z], s_z.at[which], r_z.at[which], dev(z_peer(j), yc, x))

    def seven(buf):
        return buf.at[pl.ds(0, 7)]

    w1_wait(0, win_w.at[z])

    @pl.loop(1, 8)
    def _(j):
        z_copy(0, win_w, j).start()

    w1_wait(1, wo_w.at[z])

    @pl.loop(1, 8)
    def _(j):
        z_copy(1, wo_w, j).start()

    w1_wait(2, gu_w.at[z])
    w1_wait(3, wd_w.at[z, :, pl.ds(0, 6)])

    def ring(step, way, which):
        block = lax.rem(z - (step - 1) + 8, 8) if way == 0 else lax.rem(z + step - 1, 8)
        target = lax.rem(z + 1, 8) if way == 0 else lax.rem(z + 7, 8)
        ref = gu_w.at[block] if which == 0 else wd_w.at[block, :, pl.ds(0, 6)]
        return remote(ref, ref, s_ring.at[way, step - 1, which], r_ring.at[way, step - 1, which], dev(target, yc, x))

    def ways(step):
        return (0, 1) if step < 4 else (0,)

    def ring_step(step):
        for which in range(2):
            for way in (0, 1):
                if step > 1 and way in ways(step - 1):
                    ring(step - 1, way, which).wait_recv()
            if step <= 4:
                for way in ways(step):
                    ring(step, way, which).start()

    ring_step(1)

    bias = jnp.zeros((1, 640), f32)
    tail[...] = jnp.zeros_like(tail)
    lane640 = iota((1, 640), 1)
    row_ids = iota((64, 128), 1)
    keep_all = keep_ref[...]
    for p in range(8):
        picks = (keep_all[:, p:p + 1] == row_ids).astype(f32)
        weight = drop_ref[p:p + 1, :] * (1.0 - jnp.sum(picks, axis=0, keepdims=True))
        total = jnp.sum(weight, axis=1, keepdims=True)
        w1 = rounded(weight)
        w2 = rounded(weight - w1)
        w3 = weight - w1 - w2
        left = jnp.concatenate([picks, w1, w2, w3, jnp.zeros((13, 128), f32)], axis=0).astype(bf16)
        got = dot(left, cache_ref[p])
        kv[p] = got[0:64].astype(bf16)
        mean = rounded((got[64:65] + got[65:66] + got[66:67]) / total)
        tail[p:p + 1, :] = mean
        means[p] = mean
        bias = jnp.where(lane640 == 512 + p, jnp.log(total), bias)

    for f in range(8):
        page = inv_ref[f]
        compact_ref[f // 2, (f % 2) * 64:(f % 2) * 64 + 64, :] = kv[page]
        sumr[f:f + 1, :] = means[page]
    summary_ref[...] = sumr[...].astype(bf16)

    sel_row = iota((512, 128), 0)
    sel_col = iota((512, 128), 1)
    select = (
        ((sel_row & 127) >> 5 == yb)
        & (sel_col >> 5 == sel_row >> 7)
        & ((sel_row & 31) == (sel_col & 31))
    ).astype(bf16)

    pltpu.make_async_copy(hx.at[pl.ds(0, 3)], hx.at[pl.ds(0, 3)], r_ph.at[0]).wait()
    square = jnp.zeros((32, 1), f32)
    for k in range(4):
        part = hx[k].astype(f32)
        square += jnp.sum(part * part, axis=1, keepdims=True)
    scale = lax.rsqrt(square * (1.0 / D) + epsilon)
    pieces = []
    for k in range(4):
        normed = (hx[k].astype(f32) * scale * again_ref[:, k * 512:(k + 1) * 512]).astype(bf16)
        pieces.append(dot(normed, select).astype(bf16))
    x_in = jnp.concatenate(pieces, axis=1)

    pltpu.make_async_copy(seven(win_w), seven(win_w), r_z.at[0]).wait()
    partial = dot(x_in, win_w[...].reshape(512, 128))
    for k in range(16):
        pb[k] = partial[2 * k:2 * k + 2, :]
    rb[yc] = pb[yc]

    def b_copy(j):
        return remote(pb.at[yc_peer(j)], rb.at[yc], s_ph.at[1], r_ph.at[1], dev(z, yc_peer(j), x))

    @pl.loop(1, 16)
    def _(j):
        b_copy(j).start()

    ring_step(2)
    fifteen = pl.ds(0, 15)
    pltpu.make_async_copy(rb.at[fifteen], rb.at[fifteen], r_ph.at[1]).wait()
    for a in range(4):
        cx[x, a] = rounded(rb[4 * a] + rb[4 * a + 1] + rb[4 * a + 2] + rb[4 * a + 3])

    def c_copy(j):
        return remote(cx.at[x], cx.at[x], s_ph.at[2], r_ph.at[2], dev(z, yc, x_peer(j)))

    for j in range(1, 4):
        c_copy(j).start()
    three = pl.ds(0, 3)
    pltpu.make_async_copy(cx.at[three], cx.at[three], r_ph.at[2]).wait()
    for k in range(16):
        fa[2 * k:2 * k + 2, :] = cx[k // 4, k % 4]

    mixed = fa[...]
    row = iota((32, 128), 0)
    lane = iota((32, 128), 1)
    low = lane < 64
    block = row >> 1
    moved = pltpu.roll(pltpu.roll(mixed, 30, 0), 64, 1)
    mixed = jnp.where(((block == 3) | (block == 11)) & ~low, mixed + moved, mixed)
    sq = mixed * mixed
    ms_low = jnp.sum(jnp.where(low, sq, 0.0), axis=1, keepdims=True) * (1.0 / HD)
    ms_high = jnp.sum(jnp.where(low, 0.0, sq), axis=1, keepdims=True) * (1.0 / HD)
    inverse = jnp.where(low, lax.rsqrt(ms_low + epsilon), lax.rsqrt(ms_high + epsilon))
    place = block * 2 + jnp.where(low, 0, 1)
    gain = jnp.where(place <= 20, qgain_ref[...], kgain_ref[...])
    vec = mixed * inverse * gain
    even_row = (row & 1) == 0
    cosine = jnp.where(even_row, cos_ref[0:1, :], cos_ref[1:2, :])
    sine = jnp.where(even_row, sin_ref[0:1, :], sin_ref[1:2, :])
    first_half = (lane & 63) < 32
    rotated = jnp.where(
        first_half,
        vec * cosine - pltpu.roll(vec, 96, 1) * sine,
        vec * cosine + pltpu.roll(vec, 32, 1) * sine,
    )
    final = jnp.where(place >= 27, mixed, rounded(rotated))
    swapped = pltpu.roll(final, 64, 1)
    low2 = low[0:2]

    def two(values, b):
        return values[2 * b:2 * b + 2, :]

    tail[8:10, 0:128] = jnp.where(low2, two(swapped, 10), two(swapped, 11))
    tail[8:10, 128:256] = jnp.where(low2, two(swapped, 11), two(final, 12))
    tail[8:10, 256:384] = two(final, 13)
    tail[8:10, 384:512] = two(final, 14)
    tail[8:10, 512:640] = two(final, 15)
    kv[8, 0:16] = tail[...].astype(bf16)
    kv[8, 16:64] = jnp.zeros((48, 640), bf16)
    kv[9] = jnp.zeros((64, 640), bf16)

    lowq = low[0:QROWS]
    fq = final[0:QROWS]
    gq = swapped[0:QROWS]
    both = jnp.concatenate([jnp.where(lowq, fq, gq), jnp.where(lowq, gq, fq)], axis=0)
    nrow = 2 * QROWS

    def row_facts(width):
        at = iota((nrow, width), 0)
        second = at >= QROWS
        inside = jnp.where(second, at - QROWS, at)
        request = inside & 1
        spot = (inside >> 1) * 2 + jnp.where(second, 1, 0)
        head = jnp.where(spot <= 7, spot, spot - 1)
        valid = (spot != 8) & (spot <= 20)
        return request, head, valid

    request, head, valid = row_facts(384)
    lane384 = iota((nrow, 384), 1)
    queries = jnp.where(
        valid & (lane384 >> 6 == head >> 2), jnp.concatenate([both, both, both], axis=1), 0.0
    ).astype(bf16)
    scores = dot_t(queries, kv[:, :, 0:384].reshape(640, 384)) * (HD ** (-0.5)) + bias
    request640, _, _ = row_facts(640)
    permit = jnp.where(request640 == 0, allow_ref[0:1, :], allow_ref[1:2, :]) > 0.5
    scores = jnp.where(permit, scores, negative)
    top = jnp.max(scores, axis=1, keepdims=True)
    weight = jnp.where(permit, jnp.exp(scores - top), 0.0)
    mass = jnp.sum(weight, axis=1, keepdims=True)
    w1 = rounded(weight)
    w2 = rounded(weight - w1)
    w3 = weight - w1 - w2
    summed = dot(jnp.concatenate([w1, w2, w3], axis=0).astype(bf16), kv[:, :, 256:640].reshape(640, 384))
    summed = summed[0:nrow] + summed[nrow:2 * nrow] + summed[2 * nrow:3 * nrow]
    summed = jnp.where(lane384 >> 6 == (head >> 2) + 1, summed, 0.0)
    folded = summed[:, 0:128] + summed[:, 128:256] + summed[:, 256:384]
    folded = folded + pltpu.roll(folded, 64, 1)
    lane128 = iota((nrow, 128), 1)
    dx[x] = jnp.where(
        lane128 < 64, folded, jnp.where(lane128 == 64, mass, jnp.where(lane128 == 65, top, 0.0))
    )

    def d_copy(j):
        return remote(dx.at[x], dx.at[x], s_ph.at[3], r_ph.at[3], dev(z, yc, x_peer(j)))

    for j in range(1, 4):
        d_copy(j).start()
    ring_step(3)

    kap = iota((1, 2048), 1)
    kclass = kap >> 9
    kz = (kap >> 6) & 7
    kyh = (kap >> 5) & 1
    kc = (kap >> 4) & 1
    ki = kap & 15
    feature = 10 * (kz * 16 + (4 * kyh + kclass) * 2 + kc) + ki
    real = ki < 10
    spread = (((feature & 63) == iota((128, 2048), 0)) & real).astype(bf16)

    pltpu.make_async_copy(dx.at[three], dx.at[three], r_ph.at[3]).wait()
    parts = [dx[k] for k in range(4)]
    tops = [at_lane(part, 65) for part in parts]
    best = jnp.maximum(jnp.maximum(tops[0], tops[1]), jnp.maximum(tops[2], tops[3]))
    acc = jnp.zeros((nrow, 128), f32)
    for k in range(4):
        acc += parts[k] * jnp.exp(tops[k] - best)
    attention = jnp.where(lane128 < 64, acc / at_lane(acc, 64), 0.0).astype(bf16)
    _, head2048, valid2048 = row_facts(2048)
    spread_rows = dot(attention, spread)
    spread_rows = jnp.where(valid2048 & (head2048 == feature >> 6), spread_rows, 0.0).astype(bf16)
    pick_at = iota((8, nrow), 1)
    pick_second = jnp.where(pick_at >= QROWS, pick_at - QROWS, pick_at)
    pick = ((pick_second & 1) == iota((8, nrow), 0)).astype(bf16)
    grouped = dot(pick, spread_rows)
    for k in range(4):
        eb[k] = grouped[0:2, k * 512:(k + 1) * 512]
    ex[yc] = eb[yb]

    def e_copy(j):
        return remote(
            eb.at[lax.rem(yc_peer(j), 4)], ex.at[yc], s_ph.at[4], r_ph.at[4], dev(z, yc_peer(j), x)
        )

    @pl.loop(1, 16)
    def _(j):
        e_copy(j).start()

    ring_step(4)
    pltpu.make_async_copy(seven(wo_w), seven(wo_w), r_z.at[1]).wait()
    pltpu.make_async_copy(ex.at[fifteen], ex.at[fifteen], r_ph.at[4]).wait()
    for k in range(16):
        xa[2 * k:2 * k + 2, :] = ex[k]
    ox[yb] = dot(xa[...].astype(bf16), wo_w[...].reshape(512, 128))

    def o_copy(j):
        return remote(ox.at[yb], ox.at[yb], s_ph.at[5], r_ph.at[5], dev(z, ya * 4 + yb_peer(j), x))

    for j in range(1, 4):
        o_copy(j).start()
    pltpu.make_async_copy(ox.at[three], ox.at[three], r_ph.at[5]).wait()
    residual = jnp.zeros((32, 128), f32)
    own_rows = hx[x]
    for k in range(4):
        residual = jnp.where(ya == k, own_rows[:, k * 128:(k + 1) * 128].astype(f32), residual)
    mid = (residual + (ox[0] + ox[1] + ox[2] + ox[3])).astype(bf16)
    mx[col] = mid
    mid_f[...] = mid.astype(f32)

    def m_copy(buf, n, j):
        peer = col_peer(j)
        return remote(
            buf.at[col], buf.at[col], s_ph.at[n], r_ph.at[n], dev(z, lax.rem(peer, 4) * 4 + yb, peer // 4)
        )

    @pl.loop(1, 16)
    def _(j):
        m_copy(mx, 6, j).start()

    pltpu.make_async_copy(mx.at[fifteen], mx.at[fifteen], r_ph.at[6]).wait()
    square = jnp.zeros((32, 128), f32)
    for k in range(16):
        part = mx[k].astype(f32)
        square += part * part
    scale = lax.rsqrt(jnp.sum(square, axis=1, keepdims=True) * (1.0 / D) + epsilon)
    pieces = []
    for u in range(4):
        tiles = []
        for t in range(4):
            k = 4 * u + t
            tiles.append((mx[k].astype(f32) * scale * fgain_ref[:, k * 128:(k + 1) * 128]).astype(bf16))
        pieces.append(dot(jnp.concatenate(tiles, axis=1), select).astype(bf16))
    x_mid = jnp.concatenate(pieces, axis=1)

    ring_step(5)
    for k in range(4):
        gs[k] = dot(x_mid, gu_w[:, :, :, k * 256:(k + 1) * 256].reshape(512, 256))
    gx[yb] = gs[yb]

    def g_copy(j):
        return remote(gs.at[yb_peer(j)], gx.at[yb], s_ph.at[7], r_ph.at[7], dev(z, ya * 4 + yb_peer(j), x))

    for j in range(1, 4):
        g_copy(j).start()
    pltpu.make_async_copy(gx.at[three], gx.at[three], r_ph.at[7]).wait()
    sums = gx[0] + gx[1] + gx[2] + gx[3]
    gate_sum = sums[:, 0:128]
    ax[col] = (gate_sum / (1.0 + jnp.exp(-gate_sum)) * sums[:, 128:256]).astype(bf16)

    @pl.loop(1, 16)
    def _(j):
        m_copy(ax, 8, j).start()

    pltpu.make_async_copy(ax.at[fifteen], ax.at[fifteen], r_ph.at[8]).wait()
    whole = jnp.concatenate([ax[k] for k in range(16)], axis=1)
    down = dot(whole, wd_w[...].reshape(2048, 128))
    for k in range(4):
        ys[k] = down[8 * k:8 * k + 8, :]
    yx[yb] = ys[yb]

    def y_copy(j):
        return remote(ys.at[yb_peer(j)], yx.at[yb], s_ph.at[9], r_ph.at[9], dev(z, ya * 4 + yb_peer(j), x))

    for j in range(1, 4):
        y_copy(j).start()
    pltpu.make_async_copy(yx.at[three], yx.at[three], r_ph.at[9]).wait()
    mine = mid_f[pl.ds(pl.multiple_of(yb * 8, 8), 8), :]
    jx[c, y, z] = (mine + (yx[0] + yx[1] + yx[2] + yx[3])).astype(bf16)

    def jz_copy(j):
        return remote(jx.at[c, y, z], jx.at[c, y, z], s_ph.at[10], r_ph.at[10], dev(z_peer(j), yc, x))

    @pl.loop(1, 8)
    def _(j):
        jz_copy(j).start()

    pltpu.make_async_copy(jx.at[0, 0, pl.ds(0, 7)], jx.at[0, 0, pl.ds(0, 7)], r_ph.at[10]).wait()

    def jy_copy(j):
        return remote(
            jx.at[c, y], jx.at[c, y], s_ph.at[11], r_ph.at[11], dev(z, lax.rem(y + j, 8) * 2 + c, x)
        )

    @pl.loop(1, 8)
    def _(j):
        jy_copy(j).start()

    pltpu.make_async_copy(jx.at[0, pl.ds(0, 7)], jx.at[0, pl.ds(0, 7)], r_ph.at[11]).wait()
    last = remote(jx.at[c], jx.at[c], s_ph.at[12], r_ph.at[12], dev(z, y * 2 + 1 - c, x))
    last.start()
    last.wait_recv()
    out_ref[...] = jx[...]

    last.wait_send()

    def sent(block, sem):
        pltpu.make_async_copy(block, block, sem).wait()

    for m in range(4):
        for a in range(4):
            src, dst, which = w1_parts(a)[m]
            target = a * 4 + cls

            @pl.when(target != yc)
            def _():
                remote(src, dst, s_w1.at[which, a], r_w1.at[which], dev(z, target, x)).wait_send()

    sent(seven(win_w), s_z.at[0])
    sent(seven(wo_w), s_z.at[1])
    for step in range(1, 5):
        for which in range(2):
            for way in ways(step):
                ring(step, way, which).wait_send()
    sent(hx.at[three], s_ph.at[0])
    sent(rb.at[fifteen], s_ph.at[1])
    sent(cx.at[three], s_ph.at[2])
    sent(dx.at[three], s_ph.at[3])
    sent(ex.at[fifteen], s_ph.at[4])
    sent(ox.at[three], s_ph.at[5])
    sent(mx.at[fifteen], s_ph.at[6])
    sent(gx.at[three], s_ph.at[7])
    sent(ax.at[fifteen], s_ph.at[8])
    sent(yx.at[three], s_ph.at[9])
    sent(jx.at[0, 0, pl.ds(0, 7)], s_ph.at[10])
    sent(jx.at[0, pl.ds(0, 7)], s_ph.at[11])


def held_request(rows, source):
    half = R_DEV // 2
    position = rows % R_DEV
    slot = rows // R_DEV * half + position - half
    continued = jnp.arange(source.shape[0], dtype=i32)
    matches = source[None, :] == slot[:, None]
    owner_cont = jnp.sum(jnp.where(matches, continued[None, :], 0), axis=1)
    carried = owner_cont // half * R_DEV + half + owner_cont % half
    return jnp.where(position < half, rows, carried)


def on_device(
    hidden_in, attention_gain, query_gain, key_gain, feedforward_gain,
    input_weight, output_weight, gate_weight, up_weight, down_weight,
    old_cache, keep_rows, drop_weights, dest_slots, lengths, page_table, source,
):
    lanes = lax.axis_size("head")
    group = lax.axis_index("req")
    lane = lax.axis_index("head")
    z = group // 16
    team = held_request(z * 32 + jnp.arange(32, dtype=i32), source)
    held = held_request(group * R_DEV + jnp.arange(R_DEV, dtype=i32), source)
    held_len = lengths[held]
    half = HD // 2
    frequency = 10000.0 ** (-jnp.arange(half, dtype=f32) / half)
    angles = (held_len * PAGE).astype(f32)[:, None] * frequency[None, :]
    cosine = jnp.tile(jnp.cos(angles), (1, 4))
    sine = jnp.tile(jnp.sin(angles), (1, 4))
    fresh_ids = jnp.arange(8, dtype=i32)
    inverse = jnp.sum(
        jnp.where(dest_slots[0][None, :] == fresh_ids[:, None], fresh_ids[None, :], 0), axis=1
    )
    per_lane = NP // lanes
    table = page_table.reshape(R_DEV, per_lane, lanes)
    mine = lax.dynamic_slice_in_dim(table, lane, 1, 2)[:, :, 0]
    logical = jnp.arange(per_lane, dtype=i32) * lanes + lane
    live = logical[None, :] < held_len[:, None]
    owner = jnp.any((mine[:, :, None] == fresh_ids[None, None, :]) & live[:, :, None], axis=1)
    row_live = keep_rows >= 0
    allow_rows = (owner[:, :, None] & row_live[None]).reshape(R_DEV, 512)
    own = (jnp.arange(R_DEV)[:, None] == jnp.arange(120)[None, :]) & (lane == 0)
    allow = jnp.concatenate([allow_rows, owner, own], axis=1).astype(f32)

    vmem = pl.BlockSpec(memory_space=pltpu.VMEM)
    smem = pl.BlockSpec(memory_space=pltpu.SMEM)
    dma = pltpu.SemaphoreType.DMA

    def scratch(*shape, dtype=f32):
        return pltpu.VMEM(shape, dtype)

    compact, summaries, rows = pl.pallas_call(
        kernel,
        name="decode",
        out_shape=(
            jax.ShapeDtypeStruct((4, PAGE, KVW), bf16),
            jax.ShapeDtypeStruct((8, KVW), bf16),
            jax.ShapeDtypeStruct((2, 8, 8, 8, 128), bf16),
        ),
        in_specs=[vmem] * 10 + [smem] + [vmem] * 7,
        out_specs=(vmem, vmem, vmem),
        scratch_shapes=[
            scratch(4, 32, 512, dtype=bf16),
            scratch(4, 16, 128, dtype=bf16),
            scratch(4, 16, 128, dtype=bf16),
            scratch(4, 16, 1024, dtype=bf16),
            scratch(4, 3, 16, 128, dtype=bf16),
            scratch(8, 4, 16, 128, dtype=bf16),
            scratch(8, 4, 16, 128, dtype=bf16),
            scratch(8, 4, 16, 1024, dtype=bf16),
            scratch(8, 2, 8, 16, 128, dtype=bf16),
            scratch(16, 2, 128),
            scratch(16, 2, 128),
            scratch(4, 4, 2, 128),
            scratch(32, 128),
            scratch(10, 64, 640, dtype=bf16),
            scratch(16, 640),
            scratch(4, 2 * QROWS, 128),
            scratch(4, 2, 512),
            scratch(16, 2, 512),
            scratch(32, 512),
            scratch(4, 32, 128),
            scratch(16, 32, 128, dtype=bf16),
            scratch(32, 128),
            scratch(4, 32, 256),
            scratch(4, 32, 256),
            scratch(16, 32, 128, dtype=bf16),
            scratch(4, 8, 128),
            scratch(4, 8, 128),
            scratch(2, 8, 8, 8, 128, dtype=bf16),
            scratch(8, 640),
            scratch(8, 1, 640),
            dma((4, 4)), dma((4,)),
            dma((2,)), dma((2,)),
            dma((2, 4, 2)), dma((2, 4, 2)),
            dma((13,)), dma((13,)),
        ],
        compiler_params=pltpu.CompilerParams(
            collective_id=0, has_side_effects=True, vmem_limit_bytes=48 << 20
        ),
    )(
        hidden_in, team[:, None], input_weight, output_weight, gate_weight, up_weight, down_weight,
        old_cache, keep_rows.T, drop_weights, inverse, cosine, sine, allow,
        attention_gain[None, :], feedforward_gain[None, :],
        jnp.tile(query_gain, 2)[None, :], jnp.tile(key_gain, 2)[None, :],
    )

    requests = hidden_in.shape[0]
    everyone = jnp.arange(requests, dtype=i32)
    position = everyone % R_DEV
    part = R_DEV // 2
    cont_index = everyone // R_DEV * part + position - part
    slot_of = source[jnp.clip(cont_index, 0, source.shape[0] - 1)]
    held_row = slot_of // part * R_DEV + part + slot_of % part
    row_of = jnp.where(position < part, everyone, held_row)
    ordered = rows.reshape(2, 4, 2, 8, 8, 128).transpose(3, 2, 0, 4, 1, 5).reshape(requests, 512)
    place = (row_of[:, None] == everyone[None, :]).astype(bf16)
    result = jnp.dot(place, ordered, preferred_element_type=f32).astype(bf16)
    return (compact, summaries, result)


def solution(mesh):
    placed = (
        P(None, "head"),
        P(),
        P(),
        P(),
        P(),
        P("req", "head"),
        P("req", "head"),
        P("req", "head"),
        P("req", "head"),
        P("req", "head"),
        P(("req", "head"), None, None),
        P(("req", "head"), None),
        P(("req", "head"), None),
        P(("req", "head"), None),
        P(),
        P("req", None),
        P(),
    )
    return jax.shard_map(
        on_device,
        mesh=mesh,
        in_specs=placed,
        out_specs=(P(("req", "head"), None, None), P(("req", "head"), None), P(None, "head")),
        check_vma=False,
    )
```

time: 1290 us -> 105 us (0.08)
  waiting for transfers between devices: 674 us -> 0 us
  blocking collectives: 531 us -> 0 us
  Pallas kernels: 0 us -> 83 us
  starting transfers between devices: 21.9 us -> 0 us
  between operations: 14.5 us -> 0.79 us
  other arithmetic: 17.2 us -> 3.64 us
    psum x3 -> x0, waiting for transfers between devices: 573 us -> none  [the longest x2 371 us: project(): lax.psum(jnp.dot(inputs, weight, preferred_element_type=jnp.float32), 'req')]
    psum x1 -> x0, blocking collectives: 492 us -> none  [on_device(): mixed = lax.psum(partial_qkv, 'req').astype(jnp.bfloat16)]
    all_gather x3 -> x0, waiting for transfers between devices: 87.9 us -> none  [full_rows(): return lax.all_gather(values, 'head', axis=1, tiled=True)]
    pallas_call x0 -> x1, Pallas kernels: none -> 83 us  [on_device(): pl.pallas_call(kernel, name='decode', out_shape=(jax.ShapeDtypeStruct((4,...]
    all_gather x4 -> x0, blocking collectives: 39.3 us -> none  [the longest x3 27.1 us: joined(): gathered = jax.tree.map(lambda a: lax.all_gather(a, axis), part)]
    all_to_all x1 -> x0, starting transfers between devices: 21.7 us -> none  [on_device(): lax.all_to_all(attention, 'req', split_axis=1, concat_axis=0, tiled=True)]
  transfers between devices with their start and end apart: 7 -> 0, of which waited for: 7 -> 0; matrix products, arithmetic and copies ran while one was open for 1% -> 0% of each run, Pallas kernels for 0% -> 0%
where the time goes in v1:
time: 105 us; the launch traced here: 104 us
  Pallas kernels  83 us (79%)
  local copies, waits for them, and re-layouts  15.9 us (15%)
  other arithmetic  3.64 us (3%)
    pallas_call x1, Pallas kernels, on_device(): pl.pallas_call(kernel, name='decode', out_shape=(jax.ShapeDtypeStruct((4,...  83 us
    unnamed x27, local copies, waits for them, and re-layouts  10.3 us

profile of v1, /device:TPU:1, one launch (start us, length us, event | category | flops | bytes accessed | tf_op | source)
XLA Modules:
  0.0 104.3 jit_solution(12596221208887906554)
XLA Ops:
  0.7 0.8 select_reduce_fusion
  1.7 0.8 fusion.12
  2.5 0.6 gather_fusion
  3.3 0.8 reshape.375
  4.5 0.7 broadcast_compare_fusion
  5.7 0.8 copy.26
  6.5 0.7 tile.16
  7.2 0.7 tile.17
  8.0 0.8 select_reduce_fusion.1.inv_ref
  8.7 1.3 %copy-done.1 = bf16[8,128,640]{2,1,0:T(8,128)(2,1)S(1)} copy-done((bf16[8,128,640]{2,1,0:T(8,128)(2,1)S(1)}, bf16[8,128,640]{2,1,0:T(8,128)(2,1)}, u32[]{:S(2)}) %copy-start.1) | copy-done | bytes 1310744
  10.1 0.9 copy-done.2
  11.0 0.8 copy-done.3
  11.8 0.8 copy-done.4
  12.6 0.8 copy-done.5
  13.3 0.7 copy-done.6
  14.1 0.7 copy-done.7
  14.8 0.7 copy-done.8
  15.5 0.7 copy-done.9
  16.2 0.7 copy-done.10
  16.9 83.0 %decode.1 = (bf16[4,128,640]{2,1,0:T(8,128)(2,1)S(1)}, bf16[8,640]{1,0:T(8,128)(2,1)S(1)}, bf16[2,8,8,8,128]{4,3,2,1,0:T(8,128)(2,1)S(1)}) custom-call(bf16[256,512]{1,0:T(8,128)(2,1)S(1)} %copy-done.2, s32[32,1]{1,0:T(8,128)S(1)} %fusion.3.held_ref, bf16[16,480]{1,0:T(8,128)(2,1)S(1)} %copy-done.6, bf16[10,512]{1,0:T(8,128)(2,1)S(1)} %copy-done.7, ...), custom_call_target="tpu_custom_call" | custom-call | tf_op jit(solution)/shard_map/decode/pallas_call | solution.py:603
  100.0 1.9 %gather_fusion.1 = s32[256]{0:T(256)S(1)} fusion(s32[128]{0:T(128)S(1)} %copy-done.11, s32[1024]{0:T(1024)S(1)} %pad_clamp_fusion), kind=kCustom, calls=%fused_computation.1 | custom fusion | bytes 3072 | tf_op jit(solution)/shard_map/gather | solution.py:664
  101.9 1.0 convolution_convert_fusion
  102.9 0.8 copy.30
  103.7 0.6 copy.31
  (44 shorter events, 1.5 us)
Async XLA Ops:
  0.6 1.9 %copy-start = (s32[256]{0:T(256)S(1)}, s32[256]{0:T(256)}, u32[]{:S(2)}) copy-start(s32[256]{0:T(256)} %param.31) | copy-start | bytes 3076
  3.2 96.8 %copy-start.11 = (s32[128]{0:T(128)S(1)}, s32[128]{0:T(128)}, u32[]{:S(2)}) copy-start(s32[128]{0:T(128)} %param.33) | copy-start | bytes 1540
  8.7 1.3 %copy-start.1 = (bf16[8,128,640]{2,1,0:T(8,128)(2,1)S(1)}, bf16[8,128,640]{2,1,0:T(8,128)(2,1)}, u32[]{:S(2)}) copy-start(bf16[8,128,640]{2,1,0:T(8,128)(2,1)} %cache_ref.1) | copy-start | bytes 3932164
  10.0 0.9 copy-start.2
  11.0 0.8 copy-start.3
  11.8 0.8 copy-start.4
  12.6 0.8 copy-start.5
  13.3 0.7 copy-start.6
  14.1 0.7 copy-start.7
  14.8 0.7 copy-start.8
  15.5 0.7 copy-start.9
  16.2 0.7 copy-start.10

commit v2 on v1

--- a/solution.py
+++ b/solution.py
@@ -1,5 +1,6 @@
 import jax
 import jax.numpy as jnp
+import numpy as np
 from jax import lax
 from jax.experimental import pallas as pl
 from jax.experimental.pallas import tpu as pltpu
@@ -44,14 +45,27 @@
 
 
 def kernel(
-    hidden_ref, held_ref, win_ref, wo_ref, wg_ref, wu_ref, wd_ref,
-    cache_ref, keep_ref, drop_ref, inv_ref, cos_ref, sin_ref, allow_ref,
-    again_ref, fgain_ref, qgain_ref, kgain_ref,
+    hidden_hbm, win_hbm, wo_hbm, wg_hbm, wu_hbm, wd_hbm, cache_hbm, keep_hbm, drop_hbm, dest_hbm,
+    lengths_hbm, table_hbm, source_hbm, again_hbm, fgain_hbm, qgain_hbm, kgain_hbm, turn_hbm,
     compact_ref, summary_ref, out_ref,
+    hidden_ref, win_ref, wo_ref, wg_ref, wu_ref, wd_ref, cache_ref, keep_ref, drop_ref, dest_ref,
+    lengths_ref, table_ref, source_ref, again_ref, fgain_ref, qgain_ref, kgain_ref, turn_ref,
     hx, win_s, wo_s, gu_s, wd_s, win_w, wo_w, gu_w, wd_w,
     pb, rb, cx, fa, kv, tail, dx, eb, ex, xa, ox, mx, mid_f, gs, gx, ax, ys, yx, jx, sumr, means,
-    s_w1, r_w1, s_z, r_z, s_ring, r_ring, s_ph, r_ph,
+    s_in, s_w1, r_w1, s_z, r_z, s_ring, r_ring, s_ph, r_ph, r_j,
 ):
+    loads = [
+        pltpu.make_async_copy(src, dst, s_in.at[k])
+        for k, (src, dst) in enumerate((
+            (win_hbm, win_ref), (source_hbm, source_ref), (hidden_hbm, hidden_ref), (wo_hbm, wo_ref),
+            (wg_hbm, wg_ref), (wu_hbm, wu_ref), (wd_hbm, wd_ref), (keep_hbm, keep_ref),
+            (drop_hbm, drop_ref), (cache_hbm, cache_ref), (dest_hbm, dest_ref), (lengths_hbm, lengths_ref),
+            (table_hbm, table_ref), (again_hbm, again_ref), (fgain_hbm, fgain_ref), (qgain_hbm, qgain_ref),
+            (kgain_hbm, kgain_ref), (turn_hbm, turn_ref),
+        ))
+    ]
+    for load in loads:
+        load.start()
     group = lax.axis_index("req")
     x = lax.axis_index("head")
     z = group // 16
@@ -97,29 +111,91 @@
     def _(j):
         greet(dev(z, yc_peer(j), x))
 
-    @pl.loop(0, 12)
-    def _(j):
-        greet(dev(z, (j // 3) * 4 + yb, x_peer(1 + lax.rem(j, 3))))
+    for j in range(1, 4):
+        greet(dev(z, yc, x_peer(j)))
 
     @pl.loop(1, 8)
     def _(j):
         greet(dev(z_peer(j), yc, x))
 
+    for k in range(2):
+        loads[k].wait()
     win = win_ref[...]
     pad = jnp.zeros((16, 32), bf16)
     even = jnp.concatenate([win, pad], axis=1)
     odd = jnp.concatenate([pad, win], axis=1)
     shifted = jnp.where(lax.rem(x, 2) == 0, even, odd)
-    wo_s[...] = jnp.zeros_like(wo_s)
-    wd_s[...] = jnp.zeros_like(wd_s)
-    gu_s[...] = jnp.zeros_like(gu_s)
+    for a in range(4):
+        win_s[a] = shifted[:, a * 128:(a + 1) * 128]
+
+    source = source_ref[...].astype(f32)
+    doubling = (iota((128, 256), 1) >> 1 == iota((128, 256), 0)).astype(bf16)
+    source_of = dot(jnp.broadcast_to(source, (8, 128)).astype(bf16), doubling)
+
+    def holds(rows, first):
+        at = iota((rows, 256), 0)
+        request = iota((rows, 256), 1)
+        plain = ((at & 1) == 0) & (request == first + at)
+        origin = jnp.broadcast_to(source_of[0:1], (rows, 256))
+        carried = ((at & 1) == 1) & ((request & 1) == 1) & (origin == ((first + at) >> 1).astype(f32))
+        return plain | carried
+
+    chosen = jnp.where(holds(32, 32 * z), 1.0, 0.0).astype(bf16)
+    loads[2].wait()
+    hx[x] = dot(chosen, hidden_ref[...]).astype(bf16)
+
+    pl.semaphore_wait(barrier, 25)
+
+    def h_copy(j):
+        return remote(hx.at[x], hx.at[x], s_ph.at[0], r_ph.at[0], dev(z, yc, x_peer(j)))
+
+    cls = lax.rem(y, 4)
+    yh = y // 4
+    slot = yh * 2 + c
+
+    def w1_parts(a):
+        return (
+            (win_s.at[a], win_w.at[z, slot], 0),
+            (wo_s.at[a], wo_w.at[z, slot], 1),
+            (gu_s.at[a], gu_w.at[z, slot], 2),
+            (wd_s.at[a], wd_w.at[z, yh, pl.ds(c * 3, 3)], 3),
+        )
+
+    def w1_send(m):
+        for a in range(4):
+            src, dst, which = w1_parts(a)[m]
+            target = a * 4 + cls
+
+            @pl.when(target != yc)
+            def _():
+                remote(src, dst, s_w1.at[which, a], r_w1.at[which], dev(z, target, x)).start()
+
+            @pl.when(target == yc)
+            def _():
+                pltpu.make_async_copy(src, dst, r_w1.at[which]).start()
+
+    def w1_wait(which, block):
+        pltpu.make_async_copy(block, block, r_w1.at[which]).wait()
+
+    def z_copy(which, buf, j):
+        return remote(buf.at[z], buf.at[z], s_z.at[which], r_z.at[which], dev(z_peer(j), yc, x))
+
+    def seven(buf):
+        return buf.at[pl.ds(0, 7)]
+
+    w1_send(0)
+    for j in range(1, 4):
+        h_copy(j).start()
+
+    for k in range(3, 7):
+        loads[k].wait()
     wo_full = jnp.concatenate([wo_ref[...], jnp.zeros((6, 512), bf16)], axis=0)
     wd_full = jnp.concatenate([wd_ref[...], jnp.zeros((8, 512), bf16)], axis=0)
+    gu_s[...] = jnp.zeros_like(gu_s)
     gate = wg_ref[...]
     up = wu_ref[...]
     for a in range(4):
         lanes = slice(a * 128, (a + 1) * 128)
-        win_s[a] = shifted[:, lanes]
         wo_s[a] = wo_full[:, lanes]
         for k in range(3):
             wd_s[a, k] = wd_full[k * 16:(k + 1) * 16, lanes]
@@ -128,68 +204,8 @@
                 first = a * 320 + k * 80 + h * 40
                 gu_s[a, :, k * 256 + h * 48:k * 256 + h * 48 + 40] = gate[:, first:first + 40]
                 gu_s[a, :, k * 256 + 128 + h * 48:k * 256 + 128 + h * 48 + 40] = up[:, first:first + 40]
-
-    chosen = (held_ref[...] == iota((32, 256), 1)).astype(bf16)
-    rows_here = dot(chosen, hidden_ref[...]).astype(bf16)
-    hx[x] = rows_here
-
-    pl.semaphore_wait(barrier, 34)
-
-    def h_copy(j):
-        return remote(hx.at[x], hx.at[x], s_ph.at[0], r_ph.at[0], dev(z, yc, x_peer(j)))
-
-    cls = lax.rem(y, 4)
-    yh = y // 4
-    slot = yh * 2 + c
-
-    def w1_parts(a):
-        return (
-            (win_s.at[a], win_w.at[z, slot], 0),
-            (wo_s.at[a], wo_w.at[z, slot], 1),
-            (gu_s.at[a], gu_w.at[z, slot], 2),
-            (wd_s.at[a], wd_w.at[z, yh, pl.ds(c * 3, 3)], 3),
-        )
-
-    for m in range(4):
-        for a in range(4):
-            src, dst, which = w1_parts(a)[m]
-            target = a * 4 + cls
-
-            @pl.when(target != yc)
-            def _():
-                remote(src, dst, s_w1.at[which, a], r_w1.at[which], dev(z, target, x)).start()
-
-            @pl.when(target == yc)
-            def _():
-                pltpu.make_async_copy(src, dst, r_w1.at[which]).start()
-
-        if m == 0:
-            for j in range(1, 4):
-                h_copy(j).start()
-
-    def w1_wait(which, block):
-        pltpu.make_async_copy(block, block, r_w1.at[which]).wait()
-
-    def z_copy(which, buf, j):
-        return remote(buf.at[z], buf.at[z], s_z.at[which], r_z.at[which], dev(z_peer(j), yc, x))
-
-    def seven(buf):
-        return buf.at[pl.ds(0, 7)]
-
-    w1_wait(0, win_w.at[z])
-
-    @pl.loop(1, 8)
-    def _(j):
-        z_copy(0, win_w, j).start()
-
-    w1_wait(1, wo_w.at[z])
-
-    @pl.loop(1, 8)
-    def _(j):
-        z_copy(1, wo_w, j).start()
-
-    w1_wait(2, gu_w.at[z])
-    w1_wait(3, wd_w.at[z, :, pl.ds(0, 6)])
+    for m in range(1, 4):
+        w1_send(m)
 
     def ring(step, way, which):
         block = lax.rem(z - (step - 1) + 8, 8) if way == 0 else lax.rem(z + step - 1, 8)
@@ -209,14 +225,16 @@
                 for way in ways(step):
                     ring(step, way, which).start()
 
-    ring_step(1)
-
+    for k in range(7, 18):
+        loads[k].wait()
     bias = jnp.zeros((1, 640), f32)
     tail[...] = jnp.zeros_like(tail)
     lane640 = iota((1, 640), 1)
-    row_ids = iota((64, 128), 1)
-    keep_all = keep_ref[...]
-    for p in range(8):
+    row_ids = iota((64, 128), 1).astype(f32)
+    eye = (iota((64, 64), 0) == iota((64, 64), 1)).astype(bf16)
+    keep_all = dot_t(eye, keep_ref[...].astype(f32).astype(bf16))
+
+    def compact_page(p, bias):
         picks = (keep_all[:, p:p + 1] == row_ids).astype(f32)
         weight = drop_ref[p:p + 1, :] * (1.0 - jnp.sum(picks, axis=0, keepdims=True))
         total = jnp.sum(weight, axis=1, keepdims=True)
@@ -229,13 +247,53 @@
         mean = rounded((got[64:65] + got[65:66] + got[66:67]) / total)
         tail[p:p + 1, :] = mean
         means[p] = mean
-        bias = jnp.where(lane640 == 512 + p, jnp.log(total), bias)
-
-    for f in range(8):
-        page = inv_ref[f]
-        compact_ref[f // 2, (f % 2) * 64:(f % 2) * 64 + 64, :] = kv[page]
-        sumr[f:f + 1, :] = means[page]
-    summary_ref[...] = sumr[...].astype(bf16)
+        return jnp.where(lane640 == 512 + p, jnp.log(total), bias)
+
+    for p in range(4):
+        bias = compact_page(p, bias)
+
+    w1_wait(0, win_w.at[z])
+
+    @pl.loop(1, 8)
+    def _(j):
+        z_copy(0, win_w, j).start()
+
+    w1_wait(1, wo_w.at[z])
+
+    @pl.loop(1, 8)
+    def _(j):
+        z_copy(1, wo_w, j).start()
+
+    for p in range(4, 8):
+        bias = compact_page(p, bias)
+
+    w1_wait(2, gu_w.at[z])
+    w1_wait(3, wd_w.at[z, :, pl.ds(0, 6)])
+    ring_step(1)
+
+    own_len = jnp.sum(
+        jnp.where(holds(8, 2 * group), jnp.broadcast_to(lengths_ref[...].astype(f32), (8, 256)), 0.0),
+        axis=1, keepdims=True,
+    )[0:2]
+    cos2 = jnp.zeros((2, 128), f32)
+    sin2 = jnp.zeros((2, 128), f32)
+    for k in range(NP):
+        cos2 = jnp.where(own_len == k + 1.0, turn_ref[k:k + 1, :], cos2)
+        sin2 = jnp.where(own_len == k + 1.0, turn_ref[NP + k:NP + k + 1, :], sin2)
+    table = table_ref[...].astype(f32)
+    entry = iota((2, 640), 1)
+    page_of = jnp.where(entry < 512, entry >> 6, entry - 512).astype(f32)
+    owned = jnp.zeros((2, 640), f32)
+    for k in range(4):
+        logical = 4 * k + x
+        spot_of = jnp.sum(jnp.where(iota((2, NP), 1) == logical, table, 0.0), axis=1, keepdims=True)
+        alive = jnp.where(own_len > logical.astype(f32), 1.0, 0.0)
+        owned = jnp.where(page_of == spot_of, alive, owned)
+    listed = jnp.concatenate(
+        [keep_ref[k:k + 1, :] for k in range(8)] + [jnp.zeros((1, 128), i32)], axis=1
+    )
+    owned = jnp.where((entry < 520) & (listed >= 0), owned, 0.0)
+    allow = jnp.where((entry == 520 + iota((2, 640), 0)) & (x == 0), 1.0, owned)
 
     sel_row = iota((512, 128), 0)
     sel_col = iota((512, 128), 1)
@@ -298,11 +356,13 @@
     ms_high = jnp.sum(jnp.where(low, 0.0, sq), axis=1, keepdims=True) * (1.0 / HD)
     inverse = jnp.where(low, lax.rsqrt(ms_low + epsilon), lax.rsqrt(ms_high + epsilon))
     place = block * 2 + jnp.where(low, 0, 1)
-    gain = jnp.where(place <= 20, qgain_ref[...], kgain_ref[...])
+    qgain = jnp.concatenate([qgain_ref[...]] * 2, axis=1)
+    kgain = jnp.concatenate([kgain_ref[...]] * 2, axis=1)
+    gain = jnp.where(place <= 20, qgain, kgain)
     vec = mixed * inverse * gain
     even_row = (row & 1) == 0
-    cosine = jnp.where(even_row, cos_ref[0:1, :], cos_ref[1:2, :])
-    sine = jnp.where(even_row, sin_ref[0:1, :], sin_ref[1:2, :])
+    cosine = jnp.where(even_row, cos2[0:1, :], cos2[1:2, :])
+    sine = jnp.where(even_row, sin2[0:1, :], sin2[1:2, :])
     first_half = (lane & 63) < 32
     rotated = jnp.where(
         first_half,
@@ -348,7 +408,7 @@
     ).astype(bf16)
     scores = dot_t(queries, kv[:, :, 0:384].reshape(640, 384)) * (HD ** (-0.5)) + bias
     request640, _, _ = row_facts(640)
-    permit = jnp.where(request640 == 0, allow_ref[0:1, :], allow_ref[1:2, :]) > 0.5
+    permit = jnp.where(request640 == 0, allow[0:1, :], allow[1:2, :]) > 0.5
     scores = jnp.where(permit, scores, negative)
     top = jnp.max(scores, axis=1, keepdims=True)
     weight = jnp.where(permit, jnp.exp(scores - top), 0.0)
@@ -372,6 +432,14 @@
     for j in range(1, 4):
         d_copy(j).start()
     ring_step(3)
+
+    for f in range(8):
+        page = 0
+        for q in range(1, 8):
+            page = jnp.where(dest_ref[0, q] == f, q, page)
+        compact_ref[f // 2, (f % 2) * 64:(f % 2) * 64 + 64, :] = kv[page]
+        sumr[f:f + 1, :] = means[page]
+    summary_ref[...] = sumr[...].astype(bf16)
 
     kap = iota((1, 2048), 1)
     kclass = kap >> 9
@@ -490,33 +558,61 @@
         y_copy(j).start()
     pltpu.make_async_copy(yx.at[three], yx.at[three], r_ph.at[9]).wait()
     mine = mid_f[pl.ds(pl.multiple_of(yb * 8, 8), 8), :]
-    jx[c, y, z] = (mine + (yx[0] + yx[1] + yx[2] + yx[3])).astype(bf16)
-
-    def jz_copy(j):
-        return remote(jx.at[c, y, z], jx.at[c, y, z], s_ph.at[10], r_ph.at[10], dev(z_peer(j), yc, x))
+    outer = jnp.where(c == 0, y, z)
+    inner = jnp.where(c == 0, z, y)
+    jx[c, outer, inner] = (mine + (yx[0] + yx[1] + yx[2] + yx[3])).astype(bf16)
+
+    def along(value, first):
+        zz = jnp.where((c == 0) == first, value, z)
+        yy = jnp.where((c == 0) == first, y, value)
+        return dev(zz, yy * 2 + c, x)
+
+    mate = dev(z, y * 2 + 1 - c, x)
 
     @pl.loop(1, 8)
     def _(j):
-        jz_copy(j).start()
+        block = jx.at[c, outer, inner]
+        remote(block, block, s_ph.at[10], r_ph.at[10], along(lax.rem(inner + j, 8), True)).start()
 
     pltpu.make_async_copy(jx.at[0, 0, pl.ds(0, 7)], jx.at[0, 0, pl.ds(0, 7)], r_ph.at[10]).wait()
 
-    def jy_copy(j):
-        return remote(
-            jx.at[c, y], jx.at[c, y], s_ph.at[11], r_ph.at[11], dev(z, lax.rem(y + j, 8) * 2 + c, x)
-        )
+    def j_copy(j):
+        block = jx.at[c, outer]
+        return remote(block, block, s_ph.at[11], r_j.at[outer], along(lax.rem(outer + j, 8), False))
+
+    def m_forward(at):
+        block = jx.at[c, at]
+        return remote(block, block, s_ph.at[12], r_ph.at[12], mate)
 
     @pl.loop(1, 8)
     def _(j):
-        jy_copy(j).start()
-
-    pltpu.make_async_copy(jx.at[0, pl.ds(0, 7)], jx.at[0, pl.ds(0, 7)], r_ph.at[11]).wait()
-    last = remote(jx.at[c], jx.at[c], s_ph.at[12], r_ph.at[12], dev(z, y * 2 + 1 - c, x))
-    last.start()
-    last.wait_recv()
-    out_ref[...] = jx[...]
-
-    last.wait_send()
+        j_copy(j).start()
+
+    m_forward(outer).start()
+
+    into = (iota((256, 128), 0) >> 1 == iota((256, 128), 1)).astype(bf16)
+    group_of = dot_t(into, jnp.broadcast_to(source, (8, 128)).astype(bf16))[:, 0:1]
+    request_id = iota((256, 256), 0)
+    spot = iota((256, 256), 1)
+    held_row = ((spot >> 3) & 7) * 32 + (spot >> 7) * 16 + ((spot >> 6) & 1) * 8 + (spot & 7)
+    wanted = jnp.where((request_id & 1) == 0, request_id.astype(f32), 2.0 * group_of + 1.0)
+    back = (held_row.astype(f32) == wanted).astype(bf16)
+
+    @pl.loop(1, 8)
+    def _(j):
+        at = lax.rem(outer + 8 - j, 8)
+        block = jx.at[c, at]
+        remote(block, block, s_ph.at[11], r_j.at[at], mate).wait_recv()
+        m_forward(at).start()
+
+    pltpu.make_async_copy(jx.at[0], jx.at[0], r_ph.at[12]).wait()
+    for a in range(4):
+        blocks = []
+        for h in range(2):
+            blocks.append(jx[0, 2 * a + h].reshape(64, 128))
+            blocks.append(jx[1, :, 2 * a + h].reshape(64, 128))
+        out_ref[:, a * 128:(a + 1) * 128] = dot(back, jnp.concatenate(blocks, axis=0)).astype(bf16)
+
 
     def sent(block, sem):
         pltpu.make_async_copy(block, block, sem).wait()
@@ -548,17 +644,15 @@
     sent(yx.at[three], s_ph.at[9])
     sent(jx.at[0, 0, pl.ds(0, 7)], s_ph.at[10])
     sent(jx.at[0, pl.ds(0, 7)], s_ph.at[11])
-
-
-def held_request(rows, source):
-    half = R_DEV // 2
-    position = rows % R_DEV
-    slot = rows // R_DEV * half + position - half
-    continued = jnp.arange(source.shape[0], dtype=i32)
-    matches = source[None, :] == slot[:, None]
-    owner_cont = jnp.sum(jnp.where(matches, continued[None, :], 0), axis=1)
-    carried = owner_cont // half * R_DEV + half + owner_cont % half
-    return jnp.where(position < half, rows, carried)
+    sent(jx.at[0], s_ph.at[12])
+
+
+def rotation_table():
+    half = HD // 2
+    frequency = np.float32(10000.0) ** (-np.arange(half, dtype=np.float32) / np.float32(half))
+    positions = (PAGE * np.arange(1, NP + 1)).astype(np.float32)
+    angles = np.tile((positions[:, None] * frequency[None, :]).astype(np.float64), (1, 4))
+    return np.concatenate([np.cos(angles), np.sin(angles)], axis=0).astype(np.float32)
 
 
 def on_device(
@@ -566,51 +660,33 @@
     input_weight, output_weight, gate_weight, up_weight, down_weight,
     old_cache, keep_rows, drop_weights, dest_slots, lengths, page_table, source,
 ):
-    lanes = lax.axis_size("head")
-    group = lax.axis_index("req")
-    lane = lax.axis_index("head")
-    z = group // 16
-    team = held_request(z * 32 + jnp.arange(32, dtype=i32), source)
-    held = held_request(group * R_DEV + jnp.arange(R_DEV, dtype=i32), source)
-    held_len = lengths[held]
-    half = HD // 2
-    frequency = 10000.0 ** (-jnp.arange(half, dtype=f32) / half)
-    angles = (held_len * PAGE).astype(f32)[:, None] * frequency[None, :]
-    cosine = jnp.tile(jnp.cos(angles), (1, 4))
-    sine = jnp.tile(jnp.sin(angles), (1, 4))
-    fresh_ids = jnp.arange(8, dtype=i32)
-    inverse = jnp.sum(
-        jnp.where(dest_slots[0][None, :] == fresh_ids[:, None], fresh_ids[None, :], 0), axis=1
+    operands = (
+        hidden_in, input_weight, output_weight, gate_weight, up_weight, down_weight,
+        old_cache, keep_rows, drop_weights, dest_slots,
+        lengths[None, :], page_table, source[None, :],
+        attention_gain[None, :], feedforward_gain[None, :], query_gain[None, :], key_gain[None, :],
+        jnp.asarray(rotation_table()),
     )
-    per_lane = NP // lanes
-    table = page_table.reshape(R_DEV, per_lane, lanes)
-    mine = lax.dynamic_slice_in_dim(table, lane, 1, 2)[:, :, 0]
-    logical = jnp.arange(per_lane, dtype=i32) * lanes + lane
-    live = logical[None, :] < held_len[:, None]
-    owner = jnp.any((mine[:, :, None] == fresh_ids[None, None, :]) & live[:, :, None], axis=1)
-    row_live = keep_rows >= 0
-    allow_rows = (owner[:, :, None] & row_live[None]).reshape(R_DEV, 512)
-    own = (jnp.arange(R_DEV)[:, None] == jnp.arange(120)[None, :]) & (lane == 0)
-    allow = jnp.concatenate([allow_rows, owner, own], axis=1).astype(f32)
-
     vmem = pl.BlockSpec(memory_space=pltpu.VMEM)
-    smem = pl.BlockSpec(memory_space=pltpu.SMEM)
+    hbm = pl.BlockSpec(memory_space=pltpu.HBM)
     dma = pltpu.SemaphoreType.DMA
 
     def scratch(*shape, dtype=f32):
         return pltpu.VMEM(shape, dtype)
 
-    compact, summaries, rows = pl.pallas_call(
+    return pl.pallas_call(
         kernel,
         name="decode",
         out_shape=(
             jax.ShapeDtypeStruct((4, PAGE, KVW), bf16),
             jax.ShapeDtypeStruct((8, KVW), bf16),
-            jax.ShapeDtypeStruct((2, 8, 8, 8, 128), bf16),
+            jax.ShapeDtypeStruct(hidden_in.shape, bf16),
         ),
-        in_specs=[vmem] * 10 + [smem] + [vmem] * 7,
+        in_specs=[hbm] * len(operands),
         out_specs=(vmem, vmem, vmem),
         scratch_shapes=[
+            (pltpu.SMEM if k == 9 else pltpu.VMEM)(a.shape, a.dtype) for k, a in enumerate(operands)
+        ] + [
             scratch(4, 32, 512, dtype=bf16),
             scratch(4, 16, 128, dtype=bf16),
             scratch(4, 16, 128, dtype=bf16),
@@ -641,33 +717,16 @@
             scratch(2, 8, 8, 8, 128, dtype=bf16),
             scratch(8, 640),
             scratch(8, 1, 640),
+            dma((len(operands),)),
             dma((4, 4)), dma((4,)),
             dma((2,)), dma((2,)),
             dma((2, 4, 2)), dma((2, 4, 2)),
-            dma((13,)), dma((13,)),
+            dma((13,)), dma((13,)), dma((8,)),
         ],
         compiler_params=pltpu.CompilerParams(
-            collective_id=0, has_side_effects=True, vmem_limit_bytes=48 << 20
+            collective_id=0, has_side_effects=True, vmem_limit_bytes=63 << 20
         ),
-    )(
-        hidden_in, team[:, None], input_weight, output_weight, gate_weight, up_weight, down_weight,
-        old_cache, keep_rows.T, drop_weights, inverse, cosine, sine, allow,
-        attention_gain[None, :], feedforward_gain[None, :],
-        jnp.tile(query_gain, 2)[None, :], jnp.tile(key_gain, 2)[None, :],
-    )
-
-    requests = hidden_in.shape[0]
-    everyone = jnp.arange(requests, dtype=i32)
-    position = everyone % R_DEV
-    part = R_DEV // 2
-    cont_index = everyone // R_DEV * part + position - part
-    slot_of = source[jnp.clip(cont_index, 0, source.shape[0] - 1)]
-    held_row = slot_of // part * R_DEV + part + slot_of % part
-    row_of = jnp.where(position < part, everyone, held_row)
-    ordered = rows.reshape(2, 4, 2, 8, 8, 128).transpose(3, 2, 0, 4, 1, 5).reshape(requests, 512)
-    place = (row_of[:, None] == everyone[None, :]).astype(bf16)
-    result = jnp.dot(place, ordered, preferred_element_type=f32).astype(bf16)
-    return (compact, summaries, result)
+    )(*operands)
 
 
 def solution(mesh):

time: 105 us -> 86.1 us (0.82)
  local copies, waits for them, and re-layouts: 15.9 us -> 3.33 us
  other arithmetic: 3.64 us -> 0 us
  Pallas kernels: 83 us -> 81.9 us
    unnamed x27 -> x7, local copies, waits for them, and re-layouts: 10.3 us -> 3.33 us
    gather x2 -> x0, local copies, waits for them, and re-layouts: 2.51 us -> none  [the longest x1 1.87 us: on_device(): slot_of = source[jnp.clip(cont_index, 0, source.shape[0] - 1)]]
    reduce_sum x3 -> x0, other arithmetic: 2.44 us -> none  [the longest x2 1.67 us: held_request(): owner_cont = jnp.sum(jnp.where(matches, continued[None, :], 0), axis=1)]
    another operation x8 -> x0, local copies, waits for them, and re-layouts: 1.65 us -> none  [the longest x2 0.74 us: on_device(): jnp.tile(key_gain, 2)[None, :]]
    pallas_call x1, Pallas kernels: 83 us -> 81.9 us  [on_device(): pl.pallas_call(kernel, name='decode', out_shape=(jax.ShapeDtypeStruct((4,...]
where the time goes in v2:
time: 86.1 us; the launch traced here: 85.9 us
  Pallas kernels  81.9 us (95%)
  local copies, waits for them, and re-layouts  3.33 us (4%)
    pallas_call x1, Pallas kernels, on_device(): pl.pallas_call(kernel, name='decode', out_shape=(jax.ShapeDtypeStruct((4,...  81.9 us
    unnamed x7, local copies, waits for them, and re-layouts  3.33 us

profile of v2, /device:TPU:1, one launch (start us, length us, event | category | flops | bytes accessed | tf_op | source)
XLA Modules:
  0.0 85.9 jit_solution(7552180171851872503)
XLA Ops:
  0.6 81.9 %decode.1 = (bf16[4,128,640]{2,1,0:T(8,128)(2,1)}, bf16[8,640]{1,0:T(8,128)(2,1)}, bf16[256,512]{1,0:T(8,128)(2,1)}) custom-call(bf16[256,512]{1,0:T(8,128)(2,1)} %hidden_hbm.1, bf16[16,480]{1,0:T(8,128)(2,1)} %win_hbm.1, bf16[10,512]{1,0:T(8,128)(2,1)} %wo_hbm.1, bf16[16,1280]{1,0:T(8,128)(2,1)} %wg_hbm.1, bf16[16,1280]{1,0:T(8,128)(2,1)} %wu_hbm.1, ...), custom_call_target="tpu_custom_call" | custom-call | tf_op jit(solution)/shard_map/decode/pallas_call | solution.py:677
  82.6 0.0 copy-start.1
  82.6 0.0 copy-start
  82.6 2.0 %copy.24 = bf16[4,128,640]{2,1,0:T(8,128)(2,1)} copy(bf16[4,128,640]{2,1,0:T(8,128)(2,1)} %get-tuple-element.6) | data formatting | bytes 1310720
  84.6 0.0 copy-done.1
  84.6 0.6 copy.25
  85.2 0.0 copy-done
  85.2 0.7 copy.26
Async XLA Ops:
  82.6 2.0 %copy-start.1 = (bf16[8,640]{1,0:T(8,128)(2,1)S(1)}, bf16[8,640]{1,0:T(8,128)(2,1)}, u32[]{:S(2)}) copy-start(bf16[8,640]{1,0:T(8,128)(2,1)} %get-tuple-element.7) | copy-start | bytes 30724
  82.6 2.6 %copy-start = (bf16[256,512]{1,0:T(8,128)(2,1)S(1)}, bf16[256,512]{1,0:T(8,128)(2,1)}, u32[]{:S(2)}) copy-start(bf16[256,512]{1,0:T(8,128)(2,1)} %get-tuple-element.8) | copy-start | bytes 786436

commit v3 on v2

--- a/solution.py
+++ b/solution.py
@@ -47,12 +47,12 @@
 def kernel(
     hidden_hbm, win_hbm, wo_hbm, wg_hbm, wu_hbm, wd_hbm, cache_hbm, keep_hbm, drop_hbm, dest_hbm,
     lengths_hbm, table_hbm, source_hbm, again_hbm, fgain_hbm, qgain_hbm, kgain_hbm, turn_hbm,
-    compact_ref, summary_ref, out_ref,
+    compact_hbm, summary_hbm, out_hbm,
     hidden_ref, win_ref, wo_ref, wg_ref, wu_ref, wd_ref, cache_ref, keep_ref, drop_ref, dest_ref,
     lengths_ref, table_ref, source_ref, again_ref, fgain_ref, qgain_ref, kgain_ref, turn_ref,
     hx, win_s, wo_s, gu_s, wd_s, win_w, wo_w, gu_w, wd_w,
-    pb, rb, cx, fa, kv, tail, dx, eb, ex, xa, ox, mx, mid_f, gs, gx, ax, ys, yx, jx, sumr, means,
-    s_in, s_w1, r_w1, s_z, r_z, s_ring, r_ring, s_ph, r_ph, r_j,
+    pb, rb, cx, fa, kv, tail, dx, eb, ex, xa, ox, mx, mid_f, ax, ys, yx, jx, sumr, means, compact_ref, summary_ref, out_ref,
+    s_in, s_out, s_w1, r_w1, s_z, r_z, s_ring, r_ring, s_ph, r_ph, r_j,
 ):
     loads = [
         pltpu.make_async_copy(src, dst, s_in.at[k])
@@ -157,8 +157,7 @@
         return (
             (win_s.at[a], win_w.at[z, slot], 0),
             (wo_s.at[a], wo_w.at[z, slot], 1),
-            (gu_s.at[a], gu_w.at[z, slot], 2),
-            (wd_s.at[a], wd_w.at[z, yh, pl.ds(c * 3, 3)], 3),
+            (wd_s.at[a], wd_w.at[z, yh, pl.ds(c * 3, 3)], 2),
         )
 
     def w1_send(m):
@@ -202,10 +201,14 @@
         for k in range(4):
             for h in range(2):
                 first = a * 320 + k * 80 + h * 40
-                gu_s[a, :, k * 256 + h * 48:k * 256 + h * 48 + 40] = gate[:, first:first + 40]
-                gu_s[a, :, k * 256 + 128 + h * 48:k * 256 + 128 + h * 48 + 40] = up[:, first:first + 40]
-    for m in range(1, 4):
-        w1_send(m)
+                gu_s[a * 4 + k, :, h * 48:h * 48 + 40] = gate[:, first:first + 40]
+                gu_s[a * 4 + k, :, 128 + h * 48:128 + h * 48 + 40] = up[:, first:first + 40]
+    w1_send(1)
+    gu_w[z, yc] = gu_s[yc]
+
+    def gu_copy(j):
+        return remote(gu_s.at[yc_peer(j)], gu_w.at[z, yc], s_ph.at[7], r_ph.at[7], dev(z, yc_peer(j), x))
+
 
     def ring(step, way, which):
         block = lax.rem(z - (step - 1) + 8, 8) if way == 0 else lax.rem(z + step - 1, 8)
@@ -264,11 +267,16 @@
     def _(j):
         z_copy(1, wo_w, j).start()
 
+    @pl.loop(1, 16)
+    def _(j):
+        gu_copy(j).start()
+
+    w1_send(2)
     for p in range(4, 8):
         bias = compact_page(p, bias)
 
-    w1_wait(2, gu_w.at[z])
-    w1_wait(3, wd_w.at[z, :, pl.ds(0, 6)])
+    pltpu.make_async_copy(gu_w.at[z, pl.ds(0, 15)], gu_w.at[z, pl.ds(0, 15)], r_ph.at[7]).wait()
+    w1_wait(2, wd_w.at[z, :, pl.ds(0, 6)])
     ring_step(1)
 
     own_len = jnp.sum(
@@ -440,6 +448,13 @@
         compact_ref[f // 2, (f % 2) * 64:(f % 2) * 64 + 64, :] = kv[page]
         sumr[f:f + 1, :] = means[page]
     summary_ref[...] = sumr[...].astype(bf16)
+    stores = [
+        pltpu.make_async_copy(compact_ref, compact_hbm, s_out.at[0]),
+        pltpu.make_async_copy(summary_ref, summary_hbm, s_out.at[1]),
+        pltpu.make_async_copy(out_ref, out_hbm, s_out.at[2]),
+    ]
+    stores[0].start()
+    stores[1].start()
 
     kap = iota((1, 2048), 1)
     kclass = kap >> 9
@@ -516,27 +531,13 @@
         part = mx[k].astype(f32)
         square += part * part
     scale = lax.rsqrt(jnp.sum(square, axis=1, keepdims=True) * (1.0 / D) + epsilon)
-    pieces = []
-    for u in range(4):
-        tiles = []
-        for t in range(4):
-            k = 4 * u + t
-            tiles.append((mx[k].astype(f32) * scale * fgain_ref[:, k * 128:(k + 1) * 128]).astype(bf16))
-        pieces.append(dot(jnp.concatenate(tiles, axis=1), select).astype(bf16))
-    x_mid = jnp.concatenate(pieces, axis=1)
+    tiles = []
+    for k in range(16):
+        tiles.append((mx[k].astype(f32) * scale * fgain_ref[:, k * 128:(k + 1) * 128]).astype(bf16))
+    x_mid = jnp.concatenate(tiles, axis=1)
 
     ring_step(5)
-    for k in range(4):
-        gs[k] = dot(x_mid, gu_w[:, :, :, k * 256:(k + 1) * 256].reshape(512, 256))
-    gx[yb] = gs[yb]
-
-    def g_copy(j):
-        return remote(gs.at[yb_peer(j)], gx.at[yb], s_ph.at[7], r_ph.at[7], dev(z, ya * 4 + yb_peer(j), x))
-
-    for j in range(1, 4):
-        g_copy(j).start()
-    pltpu.make_async_copy(gx.at[three], gx.at[three], r_ph.at[7]).wait()
-    sums = gx[0] + gx[1] + gx[2] + gx[3]
+    sums = dot(x_mid, gu_w[...].reshape(2048, 256))
     gate_sum = sums[:, 0:128]
     ax[col] = (gate_sum / (1.0 + jnp.exp(-gate_sum)) * sums[:, 128:256]).astype(bf16)
 
@@ -613,11 +614,13 @@
             blocks.append(jx[1, :, 2 * a + h].reshape(64, 128))
         out_ref[:, a * 128:(a + 1) * 128] = dot(back, jnp.concatenate(blocks, axis=0)).astype(bf16)
 
+    stores[2].start()
+
 
     def sent(block, sem):
         pltpu.make_async_copy(block, block, sem).wait()
 
-    for m in range(4):
+    for m in range(3):
         for a in range(4):
             src, dst, which = w1_parts(a)[m]
             target = a * 4 + cls
@@ -639,12 +642,25 @@
     sent(ex.at[fifteen], s_ph.at[4])
     sent(ox.at[three], s_ph.at[5])
     sent(mx.at[fifteen], s_ph.at[6])
-    sent(gx.at[three], s_ph.at[7])
+    sent(gu_w.at[z, pl.ds(0, 15)], s_ph.at[7])
     sent(ax.at[fifteen], s_ph.at[8])
     sent(yx.at[three], s_ph.at[9])
     sent(jx.at[0, 0, pl.ds(0, 7)], s_ph.at[10])
     sent(jx.at[0, pl.ds(0, 7)], s_ph.at[11])
     sent(jx.at[0], s_ph.at[12])
+    for store in stores:
+        store.wait()
+
+
+def hand_over(a_ref, b_ref, c_ref, a_out, b_out, c_out, sem):
+    copies = [
+        pltpu.make_async_copy(src, dst, sem.at[k])
+        for k, (src, dst) in enumerate(((a_ref, a_out), (b_ref, b_out), (c_ref, c_out)))
+    ]
+    for copy in copies:
+        copy.start()
+    for copy in copies:
+        copy.wait()
 
 
 def rotation_table():
@@ -667,14 +683,13 @@
         attention_gain[None, :], feedforward_gain[None, :], query_gain[None, :], key_gain[None, :],
         jnp.asarray(rotation_table()),
     )
-    vmem = pl.BlockSpec(memory_space=pltpu.VMEM)
     hbm = pl.BlockSpec(memory_space=pltpu.HBM)
     dma = pltpu.SemaphoreType.DMA
 
     def scratch(*shape, dtype=f32):
         return pltpu.VMEM(shape, dtype)
 
-    return pl.pallas_call(
+    results = pl.pallas_call(
         kernel,
         name="decode",
         out_shape=(
@@ -683,18 +698,18 @@
             jax.ShapeDtypeStruct(hidden_in.shape, bf16),
         ),
         in_specs=[hbm] * len(operands),
-        out_specs=(vmem, vmem, vmem),
+        out_specs=(hbm, hbm, hbm),
         scratch_shapes=[
             (pltpu.SMEM if k == 9 else pltpu.VMEM)(a.shape, a.dtype) for k, a in enumerate(operands)
         ] + [
             scratch(4, 32, 512, dtype=bf16),
             scratch(4, 16, 128, dtype=bf16),
             scratch(4, 16, 128, dtype=bf16),
-            scratch(4, 16, 1024, dtype=bf16),
+            scratch(16, 16, 256, dtype=bf16),
             scratch(4, 3, 16, 128, dtype=bf16),
             scratch(8, 4, 16, 128, dtype=bf16),
             scratch(8, 4, 16, 128, dtype=bf16),
-            scratch(8, 4, 16, 1024, dtype=bf16),
+            scratch(8, 16, 16, 256, dtype=bf16),
             scratch(8, 2, 8, 16, 128, dtype=bf16),
             scratch(16, 2, 128),
             scratch(16, 2, 128),
@@ -709,16 +724,17 @@
             scratch(4, 32, 128),
             scratch(16, 32, 128, dtype=bf16),
             scratch(32, 128),
-            scratch(4, 32, 256),
-            scratch(4, 32, 256),
             scratch(16, 32, 128, dtype=bf16),
             scratch(4, 8, 128),
             scratch(4, 8, 128),
             scratch(2, 8, 8, 8, 128, dtype=bf16),
             scratch(8, 640),
             scratch(8, 1, 640),
-            dma((len(operands),)),
-            dma((4, 4)), dma((4,)),
+            scratch(4, PAGE, KVW, dtype=bf16),
+            scratch(8, KVW, dtype=bf16),
+            scratch(*hidden_in.shape, dtype=bf16),
+            dma((len(operands),)), dma((3,)),
+            dma((3, 4)), dma((3,)),
             dma((2,)), dma((2,)),
             dma((2, 4, 2)), dma((2, 4, 2)),
             dma((13,)), dma((13,)), dma((8,)),
@@ -727,6 +743,14 @@
             collective_id=0, has_side_effects=True, vmem_limit_bytes=63 << 20
         ),
     )(*operands)
+    return pl.pallas_call(
+        hand_over,
+        name="hand_over",
+        out_shape=tuple(jax.ShapeDtypeStruct(a.shape, a.dtype) for a in results),
+        in_specs=[hbm] * 3,
+        out_specs=(pl.BlockSpec(memory_space=pltpu.VMEM),) * 3,
+        scratch_shapes=[dma((3,))],
+    )(*results)
 
 
 def solution(mesh):

time: 86.1 us -> 82.8 us (0.962)
  local copies, waits for them, and re-layouts: 3.33 us -> 0 us
    unnamed x7 -> x0, local copies, waits for them, and re-layouts: 3.33 us -> none
    pallas_call x0 -> x1, Pallas kernels: none -> 2.11 us  [on_device(): pl.pallas_call(hand_over, name='hand_over', out_shape=tuple((jax.ShapeDty...]
    pallas_call x1, Pallas kernels: 81.9 us -> 79.9 us  [on_device(): pl.pallas_call(kernel, name='decode', out_shape=(jax.ShapeDtypeStruct((4,...]
where the time goes in v3:
time: 82.8 us; the launch traced here: 82.7 us
  Pallas kernels  82 us (99%)
    pallas_call x1, Pallas kernels, on_device(): pl.pallas_call(kernel, name='decode', out_shape=(jax.ShapeDtypeStruct((4,...  79.9 us
    pallas_call x1, Pallas kernels, on_device(): pl.pallas_call(hand_over, name='hand_over', out_shape=tuple((jax.ShapeDty...  2.11 us

profile of v3, /device:TPU:1, one launch (start us, length us, event | category | flops | bytes accessed | tf_op | source)
XLA Modules:
  0.0 82.7 jit_solution(3402697013832584648)
XLA Ops:
  0.6 79.9 %decode.1 = (bf16[4,128,640]{2,1,0:T(8,128)(2,1)}, bf16[8,640]{1,0:T(8,128)(2,1)}, bf16[256,512]{1,0:T(8,128)(2,1)}) custom-call(bf16[256,512]{1,0:T(8,128)(2,1)} %hidden_hbm.1, bf16[16,480]{1,0:T(8,128)(2,1)} %win_hbm.1, bf16[10,512]{1,0:T(8,128)(2,1)} %wo_hbm.1, bf16[16,1280]{1,0:T(8,128)(2,1)} %wg_hbm.1, bf16[16,1280]{1,0:T(8,128)(2,1)} %wu_hbm.1, ...), custom_call_target="tpu_custom_call" | custom-call | tf_op jit(solution)/shard_map/decode/pallas_call | solution.py:692
  80.5 2.1 %hand_over.1 = (bf16[4,128,640]{2,1,0:T(8,128)(2,1)}, bf16[8,640]{1,0:T(8,128)(2,1)}, bf16[256,512]{1,0:T(8,128)(2,1)}) custom-call(bf16[4,128,640]{2,1,0:T(8,128)(2,1)} %get-tuple-element.6.a_ref, bf16[8,640]{1,0:T(8,128)(2,1)} %get-tuple-element.7.b_ref, bf16[256,512]{1,0:T(8,128)(2,1)} %get-tuple-element.8.c_ref), custom_call_target="tpu_custom_call" | custom-call | tf_op jit(solution)/shard_map/hand_over/pallas_call | solution.py:746

commit v4 on v3

--- a/solution.py
+++ b/solution.py
@@ -50,7 +50,7 @@
     compact_hbm, summary_hbm, out_hbm,
     hidden_ref, win_ref, wo_ref, wg_ref, wu_ref, wd_ref, cache_ref, keep_ref, drop_ref, dest_ref,
     lengths_ref, table_ref, source_ref, again_ref, fgain_ref, qgain_ref, kgain_ref, turn_ref,
-    hx, win_s, wo_s, gu_s, wd_s, win_w, wo_w, gu_w, wd_w,
+    hx, wo_s, gu_s, wd_s, win_w, wo_w, gu_w, wd_w,
     pb, rb, cx, fa, kv, tail, dx, eb, ex, xa, ox, mx, mid_f, ax, ys, yx, jx, sumr, means, compact_ref, summary_ref, out_ref,
     s_in, s_out, s_w1, r_w1, s_z, r_z, s_ring, r_ring, s_ph, r_ph, r_j,
 ):
@@ -125,8 +125,7 @@
     even = jnp.concatenate([win, pad], axis=1)
     odd = jnp.concatenate([pad, win], axis=1)
     shifted = jnp.where(lax.rem(x, 2) == 0, even, odd)
-    for a in range(4):
-        win_s[a] = shifted[:, a * 128:(a + 1) * 128]
+    win_w[z] = shifted
 
     source = source_ref[...].astype(f32)
     doubling = (iota((128, 256), 1) >> 1 == iota((128, 256), 0)).astype(bf16)
@@ -155,9 +154,8 @@
 
     def w1_parts(a):
         return (
-            (win_s.at[a], win_w.at[z, slot], 0),
-            (wo_s.at[a], wo_w.at[z, slot], 1),
-            (wd_s.at[a], wd_w.at[z, yh, pl.ds(c * 3, 3)], 2),
+            (wo_s.at[a], wo_w.at[z, slot], 0),
+            (wd_s.at[a], wd_w.at[z, yh, pl.ds(c * 3, 3)], 1),
         )
 
     def w1_send(m):
@@ -182,7 +180,10 @@
     def seven(buf):
         return buf.at[pl.ds(0, 7)]
 
-    w1_send(0)
+    @pl.loop(1, 8)
+    def _(j):
+        z_copy(0, win_w, j).start()
+
     for j in range(1, 4):
         h_copy(j).start()
 
@@ -203,12 +204,16 @@
                 first = a * 320 + k * 80 + h * 40
                 gu_s[a * 4 + k, :, h * 48:h * 48 + 40] = gate[:, first:first + 40]
                 gu_s[a * 4 + k, :, 128 + h * 48:128 + h * 48 + 40] = up[:, first:first + 40]
-    w1_send(1)
+    w1_send(0)
     gu_w[z, yc] = gu_s[yc]
 
     def gu_copy(j):
         return remote(gu_s.at[yc_peer(j)], gu_w.at[z, yc], s_ph.at[7], r_ph.at[7], dev(z, yc_peer(j), x))
 
+
+    @pl.loop(1, 16)
+    def _(j):
+        gu_copy(j).start()
 
     def ring(step, way, which):
         block = lax.rem(z - (step - 1) + 8, 8) if way == 0 else lax.rem(z + step - 1, 8)
@@ -255,29 +260,19 @@
     for p in range(4):
         bias = compact_page(p, bias)
 
-    w1_wait(0, win_w.at[z])
+    w1_wait(0, wo_w.at[z])
 
     @pl.loop(1, 8)
     def _(j):
-        z_copy(0, win_w, j).start()
-
-    w1_wait(1, wo_w.at[z])
-
-    @pl.loop(1, 8)
-    def _(j):
         z_copy(1, wo_w, j).start()
 
-    @pl.loop(1, 16)
-    def _(j):
-        gu_copy(j).start()
-
-    w1_send(2)
+    w1_send(1)
+    pltpu.make_async_copy(gu_w.at[z, pl.ds(0, 15)], gu_w.at[z, pl.ds(0, 15)], r_ph.at[7]).wait()
+    w1_wait(1, wd_w.at[z, :, pl.ds(0, 6)])
+    ring_step(1)
+
     for p in range(4, 8):
         bias = compact_page(p, bias)
-
-    pltpu.make_async_copy(gu_w.at[z, pl.ds(0, 15)], gu_w.at[z, pl.ds(0, 15)], r_ph.at[7]).wait()
-    w1_wait(2, wd_w.at[z, :, pl.ds(0, 6)])
-    ring_step(1)
 
     own_len = jnp.sum(
         jnp.where(holds(8, 2 * group), jnp.broadcast_to(lengths_ref[...].astype(f32), (8, 256)), 0.0),
@@ -305,11 +300,12 @@
 
     sel_row = iota((512, 128), 0)
     sel_col = iota((512, 128), 1)
-    select = (
-        ((sel_row & 127) >> 5 == yb)
-        & (sel_col >> 5 == sel_row >> 7)
-        & ((sel_row & 31) == (sel_col & 31))
-    ).astype(bf16)
+    match = (
+        (sel_row >> 8 == (sel_col >> 4) & 1)
+        & ((sel_row >> 4) & 15 == yc)
+        & ((sel_row & 15) == (sel_col & 15))
+    )
+    selects = [(match & (sel_col >> 5 == k)).astype(bf16) for k in range(4)]
 
     pltpu.make_async_copy(hx.at[pl.ds(0, 3)], hx.at[pl.ds(0, 3)], r_ph.at[0]).wait()
     square = jnp.zeros((32, 1), f32)
@@ -317,14 +313,13 @@
         part = hx[k].astype(f32)
         square += jnp.sum(part * part, axis=1, keepdims=True)
     scale = lax.rsqrt(square * (1.0 / D) + epsilon)
-    pieces = []
+    x_in = jnp.zeros((32, 128), f32)
     for k in range(4):
         normed = (hx[k].astype(f32) * scale * again_ref[:, k * 512:(k + 1) * 512]).astype(bf16)
-        pieces.append(dot(normed, select).astype(bf16))
-    x_in = jnp.concatenate(pieces, axis=1)
+        x_in += dot(normed, selects[k])
 
     pltpu.make_async_copy(seven(win_w), seven(win_w), r_z.at[0]).wait()
-    partial = dot(x_in, win_w[...].reshape(512, 128))
+    partial = dot(x_in.astype(bf16), win_w[...].reshape(128, 512))
     for k in range(16):
         pb[k] = partial[2 * k:2 * k + 2, :]
     rb[yc] = pb[yc]
@@ -339,8 +334,12 @@
     ring_step(2)
     fifteen = pl.ds(0, 15)
     pltpu.make_async_copy(rb.at[fifteen], rb.at[fifteen], r_ph.at[1]).wait()
+    whole_qkv = rb[0]
+    for k in range(1, 16):
+        whole_qkv += rb[k]
+    whole_qkv = rounded(whole_qkv)
     for a in range(4):
-        cx[x, a] = rounded(rb[4 * a] + rb[4 * a + 1] + rb[4 * a + 2] + rb[4 * a + 3])
+        cx[x, a] = whole_qkv[:, a * 128:(a + 1) * 128]
 
     def c_copy(j):
         return remote(cx.at[x], cx.at[x], s_ph.at[2], r_ph.at[2], dev(z, yc, x_peer(j)))
@@ -348,55 +347,19 @@
     for j in range(1, 4):
         c_copy(j).start()
     three = pl.ds(0, 3)
-    pltpu.make_async_copy(cx.at[three], cx.at[three], r_ph.at[2]).wait()
-    for k in range(16):
-        fa[2 * k:2 * k + 2, :] = cx[k // 4, k % 4]
-
-    mixed = fa[...]
     row = iota((32, 128), 0)
     lane = iota((32, 128), 1)
     low = lane < 64
     block = row >> 1
-    moved = pltpu.roll(pltpu.roll(mixed, 30, 0), 64, 1)
-    mixed = jnp.where(((block == 3) | (block == 11)) & ~low, mixed + moved, mixed)
-    sq = mixed * mixed
-    ms_low = jnp.sum(jnp.where(low, sq, 0.0), axis=1, keepdims=True) * (1.0 / HD)
-    ms_high = jnp.sum(jnp.where(low, 0.0, sq), axis=1, keepdims=True) * (1.0 / HD)
-    inverse = jnp.where(low, lax.rsqrt(ms_low + epsilon), lax.rsqrt(ms_high + epsilon))
+    joins = ((block == 3) | (block == 11)) & ~low
     place = block * 2 + jnp.where(low, 0, 1)
     qgain = jnp.concatenate([qgain_ref[...]] * 2, axis=1)
     kgain = jnp.concatenate([kgain_ref[...]] * 2, axis=1)
     gain = jnp.where(place <= 20, qgain, kgain)
-    vec = mixed * inverse * gain
     even_row = (row & 1) == 0
     cosine = jnp.where(even_row, cos2[0:1, :], cos2[1:2, :])
     sine = jnp.where(even_row, sin2[0:1, :], sin2[1:2, :])
-    first_half = (lane & 63) < 32
-    rotated = jnp.where(
-        first_half,
-        vec * cosine - pltpu.roll(vec, 96, 1) * sine,
-        vec * cosine + pltpu.roll(vec, 32, 1) * sine,
-    )
-    final = jnp.where(place >= 27, mixed, rounded(rotated))
-    swapped = pltpu.roll(final, 64, 1)
-    low2 = low[0:2]
-
-    def two(values, b):
-        return values[2 * b:2 * b + 2, :]
-
-    tail[8:10, 0:128] = jnp.where(low2, two(swapped, 10), two(swapped, 11))
-    tail[8:10, 128:256] = jnp.where(low2, two(swapped, 11), two(final, 12))
-    tail[8:10, 256:384] = two(final, 13)
-    tail[8:10, 384:512] = two(final, 14)
-    tail[8:10, 512:640] = two(final, 15)
-    kv[8, 0:16] = tail[...].astype(bf16)
-    kv[8, 16:64] = jnp.zeros((48, 640), bf16)
-    kv[9] = jnp.zeros((64, 640), bf16)
-
-    lowq = low[0:QROWS]
-    fq = final[0:QROWS]
-    gq = swapped[0:QROWS]
-    both = jnp.concatenate([jnp.where(lowq, fq, gq), jnp.where(lowq, gq, fq)], axis=0)
+    sine = jnp.where((lane & 63) < 32, -sine, sine)
     nrow = 2 * QROWS
 
     def row_facts(width):
@@ -411,12 +374,50 @@
 
     request, head, valid = row_facts(384)
     lane384 = iota((nrow, 384), 1)
+    asks = valid & (lane384 >> 6 == head >> 2)
+    gets = lane384 >> 6 == (head >> 2) + 1
+    request640, _, _ = row_facts(640)
+    permit = jnp.where(request640 == 0, allow[0:1, :], allow[1:2, :]) > 0.5
+    lane128 = iota((nrow, 128), 1)
+    kv[9] = jnp.zeros((64, 640), bf16)
+    kv[8, 16:64] = jnp.zeros((48, 640), bf16)
+
+    pltpu.make_async_copy(cx.at[three], cx.at[three], r_ph.at[2]).wait()
+    for k in range(16):
+        fa[2 * k:2 * k + 2, :] = cx[k // 4, k % 4]
+
+    mixed = fa[...]
+    moved = pltpu.roll(pltpu.roll(mixed, 30, 0), 64, 1)
+    mixed = jnp.where(joins, mixed + moved, mixed)
+    sq = mixed * mixed
+    ms_low = jnp.sum(jnp.where(low, sq, 0.0), axis=1, keepdims=True) * (1.0 / HD)
+    ms_high = jnp.sum(jnp.where(low, 0.0, sq), axis=1, keepdims=True) * (1.0 / HD)
+    inverse = jnp.where(low, lax.rsqrt(ms_low + epsilon), lax.rsqrt(ms_high + epsilon))
+    vec = mixed * inverse * gain
+    partner = jnp.where((lane & 63) < 32, pltpu.roll(vec, 96, 1), pltpu.roll(vec, 32, 1))
+    rotated = vec * cosine + partner * sine
+    final = jnp.where(place >= 27, mixed, rounded(rotated))
+    swapped = pltpu.roll(final, 64, 1)
+    low2 = low[0:2]
+
+    def two(values, b):
+        return values[2 * b:2 * b + 2, :]
+
+    tail[8:10, 0:128] = jnp.where(low2, two(swapped, 10), two(swapped, 11))
+    tail[8:10, 128:256] = jnp.where(low2, two(swapped, 11), two(final, 12))
+    tail[8:10, 256:384] = two(final, 13)
+    tail[8:10, 384:512] = two(final, 14)
+    tail[8:10, 512:640] = two(final, 15)
+    kv[8, 0:16] = tail[...].astype(bf16)
+
+    lowq = low[0:QROWS]
+    fq = final[0:QROWS]
+    gq = swapped[0:QROWS]
+    both = jnp.concatenate([jnp.where(lowq, fq, gq), jnp.where(lowq, gq, fq)], axis=0)
     queries = jnp.where(
-        valid & (lane384 >> 6 == head >> 2), jnp.concatenate([both, both, both], axis=1), 0.0
+        asks, jnp.concatenate([both, both, both], axis=1), 0.0
     ).astype(bf16)
     scores = dot_t(queries, kv[:, :, 0:384].reshape(640, 384)) * (HD ** (-0.5)) + bias
-    request640, _, _ = row_facts(640)
-    permit = jnp.where(request640 == 0, allow[0:1, :], allow[1:2, :]) > 0.5
     scores = jnp.where(permit, scores, negative)
     top = jnp.max(scores, axis=1, keepdims=True)
     weight = jnp.where(permit, jnp.exp(scores - top), 0.0)
@@ -426,10 +427,9 @@
     w3 = weight - w1 - w2
     summed = dot(jnp.concatenate([w1, w2, w3], axis=0).astype(bf16), kv[:, :, 256:640].reshape(640, 384))
     summed = summed[0:nrow] + summed[nrow:2 * nrow] + summed[2 * nrow:3 * nrow]
-    summed = jnp.where(lane384 >> 6 == (head >> 2) + 1, summed, 0.0)
+    summed = jnp.where(gets, summed, 0.0)
     folded = summed[:, 0:128] + summed[:, 128:256] + summed[:, 256:384]
     folded = folded + pltpu.roll(folded, 64, 1)
-    lane128 = iota((nrow, 128), 1)
     dx[x] = jnp.where(
         lane128 < 64, folded, jnp.where(lane128 == 64, mass, jnp.where(lane128 == 65, top, 0.0))
     )
@@ -466,6 +466,11 @@
     real = ki < 10
     spread = (((feature & 63) == iota((128, 2048), 0)) & real).astype(bf16)
 
+    _, head2048, valid2048 = row_facts(2048)
+    belongs = valid2048 & (head2048 == feature >> 6)
+    pick_at = iota((8, nrow), 1)
+    pick_second = jnp.where(pick_at >= QROWS, pick_at - QROWS, pick_at)
+    pick = ((pick_second & 1) == iota((8, nrow), 0)).astype(bf16)
     pltpu.make_async_copy(dx.at[three], dx.at[three], r_ph.at[3]).wait()
     parts = [dx[k] for k in range(4)]
     tops = [at_lane(part, 65) for part in parts]
@@ -474,12 +479,8 @@
     for k in range(4):
         acc += parts[k] * jnp.exp(tops[k] - best)
     attention = jnp.where(lane128 < 64, acc / at_lane(acc, 64), 0.0).astype(bf16)
-    _, head2048, valid2048 = row_facts(2048)
     spread_rows = dot(attention, spread)
-    spread_rows = jnp.where(valid2048 & (head2048 == feature >> 6), spread_rows, 0.0).astype(bf16)
-    pick_at = iota((8, nrow), 1)
-    pick_second = jnp.where(pick_at >= QROWS, pick_at - QROWS, pick_at)
-    pick = ((pick_second & 1) == iota((8, nrow), 0)).astype(bf16)
+    spread_rows = jnp.where(belongs, spread_rows, 0.0).astype(bf16)
     grouped = dot(pick, spread_rows)
     for k in range(4):
         eb[k] = grouped[0:2, k * 512:(k + 1) * 512]
@@ -620,7 +621,7 @@
     def sent(block, sem):
         pltpu.make_async_copy(block, block, sem).wait()
 
-    for m in range(3):
+    for m in range(2):
         for a in range(4):
             src, dst, which = w1_parts(a)[m]
             target = a * 4 + cls
@@ -652,14 +653,17 @@
         store.wait()
 
 
-def hand_over(a_ref, b_ref, c_ref, a_out, b_out, c_out, sem):
-    copies = [
-        pltpu.make_async_copy(src, dst, sem.at[k])
-        for k, (src, dst) in enumerate(((a_ref, a_out), (b_ref, b_out), (c_ref, c_out)))
-    ]
-    for copy in copies:
+def hand_over(a_ref, b_ref, c_ref, a_out, b_out, c_out, a_buf, b_buf, c_buf, sem_in, sem_out):
+    parts = [(a_ref.at[k], a_buf.at[k], a_out.at[k]) for k in range(4)]
+    parts = [(c_ref, c_buf, c_out)] + parts + [(b_ref, b_buf, b_out)]
+    ins = [pltpu.make_async_copy(src, buf, sem_in.at[k]) for k, (src, buf, _) in enumerate(parts)]
+    outs = [pltpu.make_async_copy(buf, dst, sem_out.at[k]) for k, (_, buf, dst) in enumerate(parts)]
+    for copy in ins:
         copy.start()
-    for copy in copies:
+    for arrived, leaves in zip(ins, outs):
+        arrived.wait()
+        leaves.start()
+    for copy in outs:
         copy.wait()
 
 
@@ -704,15 +708,14 @@
         ] + [
             scratch(4, 32, 512, dtype=bf16),
             scratch(4, 16, 128, dtype=bf16),
-            scratch(4, 16, 128, dtype=bf16),
             scratch(16, 16, 256, dtype=bf16),
             scratch(4, 3, 16, 128, dtype=bf16),
-            scratch(8, 4, 16, 128, dtype=bf16),
+            scratch(8, 16, 512, dtype=bf16),
             scratch(8, 4, 16, 128, dtype=bf16),
             scratch(8, 16, 16, 256, dtype=bf16),
             scratch(8, 2, 8, 16, 128, dtype=bf16),
-            scratch(16, 2, 128),
-            scratch(16, 2, 128),
+            scratch(16, 2, 512),
+            scratch(16, 2, 512),
             scratch(4, 4, 2, 128),
             scratch(32, 128),
             scratch(10, 64, 640, dtype=bf16),
@@ -734,7 +737,7 @@
             scratch(8, KVW, dtype=bf16),
             scratch(*hidden_in.shape, dtype=bf16),
             dma((len(operands),)), dma((3,)),
-            dma((3, 4)), dma((3,)),
+            dma((2, 4)), dma((2,)),
             dma((2,)), dma((2,)),
             dma((2, 4, 2)), dma((2, 4, 2)),
             dma((13,)), dma((13,)), dma((8,)),
@@ -748,8 +751,8 @@
         name="hand_over",
         out_shape=tuple(jax.ShapeDtypeStruct(a.shape, a.dtype) for a in results),
         in_specs=[hbm] * 3,
-        out_specs=(pl.BlockSpec(memory_space=pltpu.VMEM),) * 3,
-        scratch_shapes=[dma((3,))],
+        out_specs=(hbm,) * 3,
+        scratch_shapes=[pltpu.VMEM(a.shape, a.dtype) for a in results] + [dma((6,)), dma((6,))],
     )(*results)
 
 

time: 82.8 us -> 79.9 us (0.965)
  Pallas kernels: 82 us -> 79.1 us
    pallas_call x1, Pallas kernels: 79.9 us -> 77.1 us  [on_device(): pl.pallas_call(kernel, name='decode', out_shape=(jax.ShapeDtypeStruct((4,...]
where the time goes in v4:
time: 79.9 us; the launch traced here: 79.7 us
  Pallas kernels  79.1 us (99%)
    pallas_call x1, Pallas kernels, on_device(): pl.pallas_call(kernel, name='decode', out_shape=(jax.ShapeDtypeStruct((4,...  77.1 us
    pallas_call x1, Pallas kernels, on_device(): pl.pallas_call(hand_over, name='hand_over', out_shape=tuple((jax.ShapeDty...  1.98 us

profile of v4, /device:TPU:1, one launch (start us, length us, event | category | flops | bytes accessed | tf_op | source)
XLA Modules:
  0.0 79.7 jit_solution(12910345459577175868)
XLA Ops:
  0.6 77.1 %decode.1 = (bf16[4,128,640]{2,1,0:T(8,128)(2,1)}, bf16[8,640]{1,0:T(8,128)(2,1)}, bf16[256,512]{1,0:T(8,128)(2,1)}) custom-call(bf16[256,512]{1,0:T(8,128)(2,1)} %hidden_hbm.1, bf16[16,480]{1,0:T(8,128)(2,1)} %win_hbm.1, bf16[10,512]{1,0:T(8,128)(2,1)} %wo_hbm.1, bf16[16,1280]{1,0:T(8,128)(2,1)} %wg_hbm.1, bf16[16,1280]{1,0:T(8,128)(2,1)} %wu_hbm.1, ...), custom_call_target="tpu_custom_call" | custom-call | tf_op jit(solution)/shard_map/decode/pallas_call | solution.py:696
  77.8 2.0 %hand_over.1 = (bf16[4,128,640]{2,1,0:T(8,128)(2,1)}, bf16[8,640]{1,0:T(8,128)(2,1)}, bf16[256,512]{1,0:T(8,128)(2,1)}) custom-call(bf16[4,128,640]{2,1,0:T(8,128)(2,1)} %get-tuple-element.6.a_ref, bf16[8,640]{1,0:T(8,128)(2,1)} %get-tuple-element.7.b_ref, bf16[256,512]{1,0:T(8,128)(2,1)} %get-tuple-element.8.c_ref), custom_call_target="tpu_custom_call" | custom-call | tf_op jit(solution)/shard_map/hand_over/pallas_call | solution.py:749
